TPU v7x, 256 devices: a whole 4x4x8 slice. The times are simulated.
256 devices in a mesh: dp: 8 (over x, core), expert: 32 (over y, z).
Axes of the slice: x: 4, y: 4, z: 8, core: 2. Of those that a mesh axis runs over, the one named last changes fastest.
Arguments:
- out_grads: bfloat16 [32768, 3584], P(('dp', 'expert')), may hold values from -6 to 6
- route_probs: float32 [32768, 4], P(('dp', 'expert')), may hold values from 0.05 to 1
- expert_ids: int32 [32768, 4], P(('dp', 'expert')), may hold values from 0 to 31, all different within a row; in each aligned block of 128 rows (0 to 127, 128 to 255, ...) at most 24 rows name the same one
- saved_inputs: bfloat16 [32768, 4, 1024], P(('dp', 'expert')), may hold values from -0.59765625 to 0.59765625
- w_latent: bfloat16 [32, 3584, 1024], P('expert'), as said below
- block_exponents: int32 [32, 3584, 8], P('expert'), may hold values from -9 to -6, as said below
Outputs:
- input_grads: bfloat16 [32768, 4, 1024], P(('dp', 'expert'))
- weight_grads: float32 [32, 3584, 1024], P('expert', 'dp')
Inputs may be any that keep to these rules, and one draw needn't show every extreme that they name: `expert_ids`: each token names 4 different experts; the 128 tokens of one device name one expert in at most 24 slots, and some expert reaches 24. `block_exponents`: one exponent per 128 consecutive inputs of one output feature. w_latent * 2^(-exponent) lies within 0.45 of a whole number from -9 to 8.
All inputs are finite; a program needn't handle non-finite values.
Results may differ from a plain program's by a relative error of at most 0.012.
Values may be sent and summed in bfloat16 or wider, within the bound.
No kernel may reach another device: no remote copies, remote signals or barrier semaphores. Data moves between devices by JAX's collectives and lax.ppermute only.
A program may use at most 128 MiB of HBM per device.

v0:
```python
import functools

import jax
import jax.numpy as jnp
from jax import lax
from jax.experimental import pallas as pl
from jax.experimental.pallas import tpu as pltpu
from jax.sharding import Mesh, PartitionSpec as P


BLK = 128
KERNEL_VMEM = 20 << 20
META = 128


def dequantize_kernel(weight_ref, exponent_ref, out_ref):
    powers = jnp.left_shift(jnp.ones_like(exponent_ref[...]), -exponent_ref[...])
    powers = powers.astype(jnp.float32).T
    inverses = 1.0 / powers
    center = jnp.bfloat16(192.0)
    for b in range(powers.shape[1]):
        here = slice(b * BLK, (b + 1) * BLK)
        shape = (powers.shape[0], BLK)
        power = jnp.broadcast_to(powers[:, b : b + 1], shape).astype(jnp.bfloat16)
        inverse = jnp.broadcast_to(inverses[:, b : b + 1], shape).astype(jnp.bfloat16)
        shifted = weight_ref[:, here] * power + center
        shifted = jnp.clip(shifted, jnp.bfloat16(184.0), jnp.bfloat16(199.0))
        out_ref[:, here] = (shifted - center) * inverse


def dequantize(weight_one, exponent_one):
    feat, hidden = weight_one.shape
    step = 256
    return pl.pallas_call(
        dequantize_kernel,
        out_shape=jax.ShapeDtypeStruct((feat, hidden), jnp.bfloat16),
        grid=(feat // step,),
        in_specs=[
            pl.BlockSpec((step, hidden), lambda i: (i, 0)),
            pl.BlockSpec((hidden // BLK, step), lambda i: (0, i)),
        ],
        out_specs=pl.BlockSpec((step, hidden), lambda i: (i, 0)),
        cost_estimate=pl.CostEstimate(
            flops=12 * feat * hidden, bytes_accessed=4 * feat * hidden, transcendentals=0
        ),
        compiler_params=pltpu.CompilerParams(vmem_limit_bytes=KERNEL_VMEM),
        name="dequantize",
    )(weight_one, exponent_one.T)


def kept_kernel(at_ref, weight_ref, exponent_ref, out_ref):
    powers = jnp.left_shift(jnp.ones_like(exponent_ref[...]), -exponent_ref[...])
    powers = powers.astype(jnp.float32)
    for b in range(powers.shape[1]):
        here = slice(b * BLK, (b + 1) * BLK)
        codes = weight_ref[:, here].astype(jnp.float32) * powers[:, b : b + 1]
        inside = jnp.where(codes >= -8.5, jnp.where(codes <= 7.5, 1.0, 0.0), 0.0)
        out_ref[:, here] = inside.astype(jnp.bfloat16)


def kept(block, weight_one, exponents, share):
    hidden = weight_one.shape[1]
    parts = 7
    step = share // parts
    return pl.pallas_call(
        kept_kernel,
        out_shape=jax.ShapeDtypeStruct((share, hidden), jnp.bfloat16),
        grid_spec=pltpu.PrefetchScalarGridSpec(
            num_scalar_prefetch=1,
            grid=(parts,),
            in_specs=[
                pl.BlockSpec((step, hidden), lambda i, at: (at[0] * parts + i, 0)),
                pl.BlockSpec((step, hidden // BLK), lambda i, at: (i, 0)),
            ],
            out_specs=pl.BlockSpec((step, hidden), lambda i, at: (i, 0)),
        ),
        cost_estimate=pl.CostEstimate(
            flops=4 * share * hidden, bytes_accessed=4 * share * hidden, transcendentals=0
        ),
        compiler_params=pltpu.CompilerParams(vmem_limit_bytes=KERNEL_VMEM),
        name="kept",
    )(block, weight_one, exponents)


def pieces_kernel(at_ref, mine_ref, other_ref, out_ref):
    total = mine_ref[0, 0].astype(jnp.float32) + other_ref[0].astype(jnp.float32)
    out_ref[0] = total.astype(jnp.bfloat16)


def pieces_of(at, partial, other):
    nx, _, share, width = partial.shape
    return pl.pallas_call(
        pieces_kernel,
        out_shape=jax.ShapeDtypeStruct((nx, share, width), jnp.bfloat16),
        grid_spec=pltpu.PrefetchScalarGridSpec(
            num_scalar_prefetch=1,
            grid=(nx,),
            in_specs=[
                pl.BlockSpec(
                    (1, 1, share, width), lambda d, at: (lax.rem(at[0] + d, nx), at[1], 0, 0)
                ),
                pl.BlockSpec((1, share, width), lambda d, at: (lax.rem(at[0] + d, nx), 0, 0)),
            ],
            out_specs=pl.BlockSpec((1, share, width), lambda d, at: (d, 0, 0)),
        ),
        cost_estimate=pl.CostEstimate(
            flops=nx * share * width, bytes_accessed=6 * nx * share * width, transcendentals=0
        ),
        name="pieces",
    )(at, partial, other)


def pick_kernel(ny, nz, cap, topk, feat, shape, at_ref, *refs):
    refs, outs = refs[:-ny], refs[-ny:]
    sources, lo = [], 0
    for parts in shape:
        sources.append(refs[lo : lo + parts])
        lo += parts
    tok = sum(r.shape[0] for r in sources[0])
    y0, z0 = at_ref[0], at_ref[1]

    def split(j):
        g = jnp.zeros_like(j)
        for d in range(1, ny):
            g = g + (j >= d * cap).astype(jnp.int32)
        return g, j - g * cap

    def expert(g):
        y = y0 + g
        return (jnp.where(y >= ny, y - ny, y) * nz + z0).astype(jnp.float32)

    lane = lax.broadcasted_iota(jnp.int32, (tok, META), 1)
    group, slot = split(lane)
    lane_expert, lane_slot = expert(group), slot.astype(jnp.float32)
    row_expert = expert(split(lax.broadcasted_iota(jnp.int32, (META, META), 0))[0])[:, :1]
    earlier = (
        lax.broadcasted_iota(jnp.int32, (tok, tok), 1)
        < lax.broadcasted_iota(jnp.int32, (tok, tok), 0)
    )
    earlier = earlier.astype(jnp.float32).astype(jnp.bfloat16)

    for i, parts in enumerate(sources):

        def columns(lo, hi):
            got = [p[:, lo:hi] for p in parts]
            return got[0] if len(got) == 1 else jnp.concatenate(got, axis=0)

        meta_low = columns(feat, feat + META)
        meta = meta_low.astype(jnp.float32)
        hit = jnp.zeros((tok, META), jnp.float32)
        for k in range(topk):
            hit = jnp.where(meta[:, k : k + 1] == lane_expert, 1.0, hit)
        hit = jnp.where(lane < ny * cap, hit, 0.0)
        before = jnp.dot(earlier, hit.astype(jnp.bfloat16), preferred_element_type=jnp.float32)
        chosen = jnp.where(before == lane_slot, hit, 0.0)
        chosen = chosen.T.astype(jnp.bfloat16)
        info = jnp.dot(chosen, meta_low, preferred_element_type=jnp.float32)
        prob = jnp.zeros((META, 1), jnp.float32)
        for k in range(topk):
            value = info[:, topk + k : topk + k + 1]
            value = value + info[:, 2 * topk + k : 2 * topk + k + 1]
            value = value + info[:, 3 * topk + k : 3 * topk + k + 1]
            prob = jnp.where(info[:, k : k + 1] == row_expert, value, prob)
        step = 512
        for lo in range(0, feat, step):
            rows = jnp.dot(chosen, columns(lo, lo + step), preferred_element_type=jnp.float32)
            rows = rows * prob
            for d in range(ny):
                outs[d][i, :, lo : lo + step] = rows[d * cap : (d + 1) * cap].astype(jnp.bfloat16)


def pick(at, sources, ny, nz, cap, topk, feat):
    count = len(sources)
    shape = tuple(len(parts) for parts in sources)
    tok = sum(p.shape[0] for p in sources[0])
    flat = [p for parts in sources for p in parts]
    vmem = pl.BlockSpec(memory_space=pltpu.VMEM)
    return pl.pallas_call(
        functools.partial(pick_kernel, ny, nz, cap, topk, feat, shape),
        out_shape=[jax.ShapeDtypeStruct((count, cap, feat), jnp.bfloat16)] * ny,
        in_specs=[pl.BlockSpec(memory_space=pltpu.SMEM)] + [vmem] * len(flat),
        out_specs=[vmem] * ny,
        cost_estimate=pl.CostEstimate(
            flops=2 * count * META * tok * feat,
            bytes_accessed=2 * count * (tok + ny * cap) * feat,
            transcendentals=0,
        ),
        compiler_params=pltpu.CompilerParams(vmem_limit_bytes=KERNEL_VMEM),
    )(at, *flat)


def wrapped(a, size):
    return jnp.where(a >= size, a - size, jnp.where(a < 0, a + size, a))


def chunk_sources(nz):
    return [[0, 1, -1]] + [[s, -s] for s in range(2, nz // 2)] + [[nz // 2]]


def multiply_kernel(*refs):
    pieces, (weight_ref, out_ref, rows_ref, acc_ref) = refs[:-4], refs[-4:]
    i = pl.program_id(0)
    rows = [p[c] for p in pieces for c in range(p.shape[0])]
    here = jnp.concatenate(rows, axis=0)
    rows_ref[...] = here
    part = jnp.dot(here, weight_ref[...], preferred_element_type=jnp.float32)

    @pl.when(i == 0)
    def _():
        acc_ref[...] = part

    @pl.when(i > 0)
    def _():
        acc_ref[...] += part

    @pl.when(i == pl.num_programs(0) - 1)
    def _():
        out_ref[...] = acc_ref[...].astype(jnp.bfloat16)


def multiply(pieces, weight):
    cap, feat = pieces[0].shape[1:]
    rows, hidden, step = sum(p.shape[0] for p in pieces) * cap, weight.shape[1], 256
    return pl.pallas_call(
        multiply_kernel,
        out_shape=[
            jax.ShapeDtypeStruct((rows, hidden), jnp.bfloat16),
            jax.ShapeDtypeStruct((rows, feat), jnp.bfloat16),
        ],
        grid=(feat // step,),
        in_specs=[pl.BlockSpec((p.shape[0], cap, step), lambda i: (0, 0, i)) for p in pieces]
        + [pl.BlockSpec((step, hidden), lambda i: (i, 0))],
        out_specs=[
            pl.BlockSpec((rows, hidden), lambda i: (0, 0)),
            pl.BlockSpec((rows, step), lambda i: (0, i)),
        ],
        scratch_shapes=[pltpu.VMEM((rows, hidden), jnp.float32)],
        cost_estimate=pl.CostEstimate(
            flops=2 * rows * feat * hidden,
            bytes_accessed=2 * feat * (rows + hidden),
            transcendentals=0,
        ),
        name="multiply",
    )(*pieces, weight)


def to_absolute_kernel(ny, nz, cap, at_ref, *refs):
    out_ref = refs[-1]
    y0, z0 = at_ref[0], at_ref[1]
    for ref, distances in zip(refs[:-1], chunk_sources(nz), strict=True):
        for d in range(ny):
            for i, s in enumerate(distances):
                lo = (d * len(distances) + i) * cap
                out_ref[wrapped(y0 - d, ny), wrapped(z0 - s, nz)] = ref[lo : lo + cap, :]


def to_absolute(at, parts, ny, nz, cap):
    vmem = pl.BlockSpec(memory_space=pltpu.VMEM)
    width = parts[0].shape[1]
    return pl.pallas_call(
        functools.partial(to_absolute_kernel, ny, nz, cap),
        out_shape=jax.ShapeDtypeStruct((ny, nz, cap, width), jnp.bfloat16),
        in_specs=[pl.BlockSpec(memory_space=pltpu.SMEM)] + [vmem] * len(parts),
        out_specs=vmem,
        cost_estimate=pl.CostEstimate(
            flops=0, bytes_accessed=4 * ny * nz * cap * width, transcendentals=0
        ),
        compiler_params=pltpu.CompilerParams(vmem_limit_bytes=KERNEL_VMEM),
        name="to_absolute",
    )(at, *parts)


def to_relative_kernel(ny, nz, cap, at_ref, in_ref, out_ref):
    y0, z0 = at_ref[0], at_ref[1]
    lo = 0
    for distances in chunk_sources(nz):
        for d in range(ny):
            for s in distances:
                out_ref[lo : lo + cap, :] = in_ref[wrapped(y0 - d, ny), wrapped(z0 - s, nz)]
                lo += cap


def to_relative(at, a, ny, nz, cap):
    vmem = pl.BlockSpec(memory_space=pltpu.VMEM)
    width = a.shape[-1]
    return pl.pallas_call(
        functools.partial(to_relative_kernel, ny, nz, cap),
        out_shape=jax.ShapeDtypeStruct((ny * nz * cap, width), jnp.bfloat16),
        in_specs=[pl.BlockSpec(memory_space=pltpu.SMEM), vmem],
        out_specs=vmem,
        cost_estimate=pl.CostEstimate(
            flops=0, bytes_accessed=4 * ny * nz * cap * width, transcendentals=0
        ),
        compiler_params=pltpu.CompilerParams(vmem_limit_bytes=KERNEL_VMEM),
        name="to_relative",
    )(at, a.reshape(ny, nz, cap, width))


def shift(a, axis, size, by):
    return lax.ppermute(a, axis, [(i, (i + by) % size) for i in range(size)])


def local(out_grads, route_probs, expert_ids, saved_inputs, w_latent, block_exponents):
    nx, nc, ny, nz = (lax.axis_size(a) for a in ("x", "core", "y", "z"))
    experts = ny * nz
    tok, topk = expert_ids.shape
    feat = out_grads.shape[1]
    hidden = saved_inputs.shape[2]
    cap = tok * topk * 3 // (2 * experts)
    slots = tok * topk
    rows = experts * cap
    at = jnp.stack([lax.axis_index("y"), lax.axis_index("z")]).astype(jnp.int32)

    high = lax.reduce_precision(route_probs, 8, 7)
    rest = route_probs - high
    middle = lax.reduce_precision(rest, 8, 7)
    meta = jnp.concatenate(
        [expert_ids.astype(jnp.float32), high, middle, rest - middle], axis=1
    ).astype(jnp.bfloat16)
    meta = jnp.pad(meta, ((0, 0), (0, META - 4 * topk)))
    own = jnp.concatenate([out_grads, meta], axis=1)

    flat_ids = expert_ids.reshape(slots)
    onehot = flat_ids[:, None] == jnp.arange(experts, dtype=jnp.int32)[None, :]
    tri = (jnp.arange(slots)[:, None] > jnp.arange(slots)[None, :]).astype(jnp.bfloat16)
    before = jnp.dot(tri, onehot.astype(jnp.bfloat16), preferred_element_type=jnp.float32)
    position = jnp.sum(jnp.where(onehot, before, 0.0), axis=1).astype(jnp.int32)
    target = flat_ids * cap + position
    place = (jnp.arange(rows, dtype=jnp.int32)[:, None] == target[None, :]).astype(jnp.bfloat16)

    def exchange(a):
        return lax.all_to_all(
            a.reshape(experts, cap, a.shape[-1]), ("y", "z"), split_axis=0, concat_axis=0, tiled=True
        )

    send_inputs = jnp.dot(
        place, saved_inputs.reshape(slots, hidden), preferred_element_type=jnp.float32
    ).astype(jnp.bfloat16)

    quantized = dequantize(w_latent[0], block_exponents[0])

    share = feat // (nx * nc)
    core, x = lax.axis_index("core"), lax.axis_index("x")
    start = (x * nc + core) * share
    keep_rows = kept(
        (x * nc + core).astype(jnp.int32)[None],
        w_latent[0],
        lax.dynamic_slice_in_dim(block_exponents[0], start, share, 0),
        share,
    )

    got, backs, all_rows = [], [], []

    def deliver(*sources):
        picked = lax.optimization_barrier(pick(at, sources, ny, nz, cap, topk, feat))
        pieces = [picked[0]]
        for d in range(1, ny):
            pieces.append(shift(picked[d], "y", ny, d))
        got.append(pieces)

    def finish(name, *groups):
        group_pieces = [p for g in groups for p in got[g]]
        if name == 0:
            back, here = multiply(group_pieces, quantized)
        else:
            here = jnp.concatenate(group_pieces, axis=0).reshape(-1, feat)
            back = jnp.dot(here, quantized, preferred_element_type=jnp.float32)
            back = back.astype(jnp.bfloat16)
        all_rows.append(here)
        lo = 0
        for g in groups:
            count = sum(p.shape[0] for p in got[g]) * cap
            backs.append(back[lo : lo + count])
            lo += count

    def hop(right, left):
        right = shift(right, "z", nz, 1)
        left = shift(left, "z", nz, -1)
        return right, left

    right, left = hop(own, own)
    right, left, quantized = lax.optimization_barrier((right, left, quantized))
    deliver((own,), (right,), (left,))
    right, left = hop(right, left)
    deliver((right,), (left,))
    right, left = hop(right, left)
    deliver((right,), (left,))
    right, left = hop(right[: tok // 2], left[tok // 2 :])
    got_inputs = exchange(send_inputs)
    deliver((right, left))
    finish(0, 0, 1)
    finish(1, 2, 3)

    back = to_absolute(at, backs, ny, nz, cap)
    returned = exchange(back).reshape(rows, hidden)
    input_grads = jnp.dot(place.T, returned, preferred_element_type=jnp.float32).astype(
        jnp.bfloat16
    )

    all_grads = jnp.concatenate(all_rows, axis=0)

    partial = lax.dot_general(
        all_grads,
        to_relative(at, got_inputs, ny, nz, cap),
        (((0,), (0,)), ((), ())),
        preferred_element_type=jnp.float32,
    ).astype(jnp.bfloat16)
    partial = partial.reshape(nx, nc, share, hidden)
    other = lax.dynamic_index_in_dim(partial, 1 - core, 1, keepdims=False)
    other = shift(other, "core", nc, 1)
    pieces = pieces_of(jnp.stack([x, core]).astype(jnp.int32), partial, other)

    def wide(d, columns=slice(None)):
        return pieces[d % nx, :, columns].astype(jnp.float32)

    low, high = slice(0, hidden // 2), slice(hidden // 2, None)
    up = shift(pieces[2, :, low], "x", nx, 1)
    down = shift(pieces[2, :, high], "x", nx, -1)
    left_high = shift(pieces[1, :, high], "x", nx, 1)
    right_low = shift(pieces[-1, :, low], "x", nx, -1)
    relay_right = (wide(1, low) + up.astype(jnp.float32)).astype(jnp.bfloat16)
    relay_left = (wide(-1, high) + down.astype(jnp.float32)).astype(jnp.bfloat16)
    left_low = shift(relay_right, "x", nx, 1)
    right_high = shift(relay_left, "x", nx, -1)
    from_left = jnp.concatenate([left_low, left_high], axis=1).astype(jnp.float32)
    from_right = jnp.concatenate([right_low, right_high], axis=1).astype(jnp.float32)
    summed = wide(0) + from_left + from_right
    weight_grads = summed * keep_rows.astype(jnp.float32)
    return (input_grads.reshape(tok, topk, hidden), weight_grads[None])


def solution(mesh):
    split = Mesh(mesh.devices.reshape(4, 2, 4, 8), ("x", "core", "y", "z"))
    every = ("x", "core", "y", "z")
    placed = (
        P(every, None),
        P(every, None),
        P(every, None),
        P(every, None, None),
        P(("y", "z"), None, None),
        P(("y", "z"), None, None),
    )
    return jax.shard_map(
        local,
        mesh=split,
        in_specs=placed,
        out_specs=(P(every, None, None), P(("y", "z"), ("x", "core"), None)),
        check_vma=False,
    )
```

profile of v0, /device:TPU:4, one launch (start us, length us, event | category | flops | bytes accessed | tf_op | source)
XLA Modules:
  0.0 230.7 jit_solution(1424937778686302525)
XLA Ops:
  5.5 4.0 %collective-permute-start.1 = (bf16[128,3712]{1,0:T(8,128)(2,1)S(1)}, bf16[128,3712]{1,0:T(8,128)(2,1)S(1)}, u32[]{:S(2)}, u32[]{:S(2)}) collective-permute-start(bf16[128,3712]{1,0:T(8,128)(2,1)S(1)} %fusion.10.refs_0_), channel_id=1, source_target_pairs={{0,7},{1,0},{2,1},{3,2},{4,3},{5,4},{6,5},{7,6},{8,15},{9,8},{10,9... | collective-permute-start | bytes 2850824 | tf_op jit(solution)/shard_map/ppermute | solution.py:300
  11.8 3.4 %convolution_convert_fusion.1 = bf16[768,1024]{1,0:T(8,128)(2,1)} fusion(bf16[512,1024]{1,0:T(8,128)(2,1)} %reshape.53, s32[512]{0:T(512)S(1)} %convert_add_fusion.3), kind=kOutput, calls=%fused_computation.11 | convolution fusion | flops 806486016 | bytes 2623488 | tf_op jit(solution)/shard_map/dot_general | solution.py:336
  15.2 8.8 %all-to-all-start.1 = ((bf16[32,24,1024]{2,1,0:T(8,128)(2,1)}), bf16[32,24,1024]{2,1,0:T(8,128)(2,1)S(1)}, u32[]{:S(2)}, u32[]{:S(2)}) async-start(bf16[32,24,1024]{2,1,0:T(8,128)(2,1)} %bitcast.57), calls=%async_computation.1 | async-start | bytes 3145728 | tf_op jit(solution)/shard_map/all_to_all | solution.py:332
  24.0 3.1 %copy-done = bf16[1,3584,1024]{2,1,0:T(8,128)(2,1)S(1)} copy-done((bf16[1,3584,1024]{2,1,0:T(8,128)(2,1)S(1)}, bf16[1,3584,1024]{2,1,0:T(8,128)(2,1)}, u32[]{:S(2)}) %copy-start) | copy-done | bytes 7340056
  27.9 8.1 %dequantize.1.refs_8_ = bf16[3584,1024]{1,0:T(8,128)(2,1)S(1)} custom-call(bf16[3584,1024]{1,0:T(8,128)(2,1)S(1)} %bitcast.48, s32[8,3584]{1,0:T(8,128)S(1)} %bitcast.54), custom_call_target="tpu_custom_call" | custom-call | flops 44040192 | bytes 14680064 | tf_op jit(solution)/shard_map/dequantize/pallas_call | solution.py:34
  36.0 2.9 %copy-done.2 = bf16[3584,1024]{1,0:T(8,128)(2,1)} copy-done((bf16[3584,1024]{1,0:T(8,128)(2,1)}, bf16[3584,1024]{1,0:T(8,128)(2,1)S(1)}, u32[]{:S(2)}) %copy-start.2) | copy-done | bytes 7340056
  42.2 3.3 %shard_map.77 = (bf16[3,24,3584]{2,1,0:T(8,128)(2,1)S(1)}, bf16[3,24,3584]{2,1,0:T(8,128)(2,1)S(1)}, bf16[3,24,3584]{2,1,0:T(8,128)(2,1)S(1)}, bf16[3,24,3584]{2,1,0:T(8,128)(2,1)S(1)}) custom-call(s32[2]{0:T(128)S(1)} %pad_add_fusion.at_ref, bf16[128,3712]{1,0:T(8,128)(2,1)S(1)} %fusion.10.refs_0_, bf16[128,3712]{1,0:T(8,128)(2,1)} %collective-permute-done.refs_1_, ...), custom_call_target="tpu_custom_call" | custom-call | flops 352321536 | bytes 4816896 | tf_op jit(solution)/shard_map/pallas_call | solution.py:178
  48.1 2.7 %collective-permute-start.3 = (bf16[3,24,3584]{2,1,0:T(8,128)(2,1)S(1)}, bf16[3,24,3584]{2,1,0:T(8,128)(2,1)S(1)}, u32[]{:S(2)}, u32[]{:S(2)}) collective-permute-start(bf16[3,24,3584]{2,1,0:T(8,128)(2,1)S(1)} %get-tuple-element.27), channel_id=1, source_target_pairs={{0,16},{8,24},{16,0},{24,8},{1,17},{9,25},{17,1},{25,9},{2,18},{10... | collective-permute-start | bytes 1548296 | tf_op jit(solution)/shard_map/ppermute | solution.py:300
  52.3 32.4 %collective-permute-done.5.refs_0_ = bf16[128,3712]{1,0:T(8,128)(2,1)} collective-permute-done((bf16[128,3712]{1,0:T(8,128)(2,1)}, bf16[128,3712]{1,0:T(8,128)(2,1)}, u32[]{:S(2)}, u32[]{:S(2)}) %collective-permute-start.5) | collective-permute-done | bytes 950304 | tf_op jit(solution)/shard_map/ppermute | solution.py:300
  84.7 3.2 %collective-permute-start.11 = (bf16[128,3712]{1,0:T(8,128)(2,1)}, bf16[128,3712]{1,0:T(8,128)(2,1)S(1)}, u32[]{:S(2)}, u32[]{:S(2)}) collective-permute-start(bf16[128,3712]{1,0:T(8,128)(2,1)} %collective-permute-done.6.refs_1_), channel_id=1, source_target_pairs={{0,7},{1,0},{2,1},{3,2},{4,3},{5,4},{6,5},{7,6},{8,15},{9,8},{10,9... | collective-permute-start | bytes 2850824 | tf_op jit(solution)/shard_map/ppermute | solution.py:300
  87.9 3.8 %shard_map.78 = (bf16[2,24,3584]{2,1,0:T(8,128)(2,1)S(1)}, bf16[2,24,3584]{2,1,0:T(8,128)(2,1)}, bf16[2,24,3584]{2,1,0:T(8,128)(2,1)}, bf16[2,24,3584]{2,1,0:T(8,128)(2,1)}) custom-call(s32[2]{0:T(128)S(1)} %pad_add_fusion.at_ref, bf16[128,3712]{1,0:T(8,128)(2,1)} %collective-permute-done.5.refs_0_, bf16[128,3712]{1,0:T(8,128)(2,1)} %collective-permute-done.6.refs_1_), custom_call_target="tpu_custom_call" | custom-call | flops 234881024 | bytes 3211264 | tf_op jit(solution)/shard_map/pallas_call | solution.py:178
  94.1 2.9 %collective-permute-start.8 = (bf16[2,24,3584]{2,1,0:T(8,128)(2,1)}, bf16[2,24,3584]{2,1,0:T(8,128)(2,1)}, u32[]{:S(2)}, u32[]{:S(2)}) collective-permute-start(bf16[2,24,3584]{2,1,0:T(8,128)(2,1)} %get-tuple-element.31), channel_id=1, source_target_pairs={{0,16},{8,24},{16,0},{24,8},{1,17},{9,25},{17,1},{25,9},{2,18},{10... | collective-permute-start | bytes 1032200 | tf_op jit(solution)/shard_map/ppermute | solution.py:300
  99.1 4.7 %collective-permute-done.7.refs_5_ = bf16[2,24,3584]{2,1,0:T(8,128)(2,1)} collective-permute-done((bf16[2,24,3584]{2,1,0:T(8,128)(2,1)}, bf16[2,24,3584]{2,1,0:T(8,128)(2,1)}, u32[]{:S(2)}, u32[]{:S(2)}) %collective-permute-start.7) | collective-permute-done | bytes 344096 | tf_op jit(solution)/shard_map/ppermute | solution.py:300
  103.8 7.5 %collective-permute-done.8.refs_6_ = bf16[2,24,3584]{2,1,0:T(8,128)(2,1)} collective-permute-done((bf16[2,24,3584]{2,1,0:T(8,128)(2,1)}, bf16[2,24,3584]{2,1,0:T(8,128)(2,1)}, u32[]{:S(2)}, u32[]{:S(2)}) %collective-permute-start.8) | collective-permute-done | bytes 344096 | tf_op jit(solution)/shard_map/ppermute | solution.py:300
  111.3 15.3 %multiply.1 = (bf16[480,1024]{1,0:T(8,128)(2,1)}, bf16[480,3584]{1,0:T(8,128)(2,1)}) custom-call(bf16[3,24,3584]{2,1,0:T(8,128)(2,1)} %copy-done.4, bf16[3,24,3584]{2,1,0:T(8,128)(2,1)} %copy-done.10, bf16[3,24,3584]{2,1,0:T(8,128)(2,1)} %copy-done.11, bf16[3,24,3584]{2,1,0:T(8,128)(2,1)} %copy-done.12, bf16[2,24,3584]{2,1,0:T(8,128)(2,1)} %copy-done.5, ...), custom_call_target="tpu_custom_call" | custom-call | flops 3523215360 | bytes 10780672 | tf_op jit(solution)/shard_map/multiply/pallas_call | solution.py:224
  126.6 2.9 %shard_map.79 = (bf16[2,24,3584]{2,1,0:T(8,128)(2,1)S(1)}, bf16[2,24,3584]{2,1,0:T(8,128)(2,1)}, bf16[2,24,3584]{2,1,0:T(8,128)(2,1)}, bf16[2,24,3584]{2,1,0:T(8,128)(2,1)}) custom-call(s32[2]{0:T(128)S(1)} %pad_add_fusion.at_ref, bf16[128,3712]{1,0:T(8,128)(2,1)S(1)} %collective-permute-done.10.refs_0_, bf16[128,3712]{1,0:T(8,128)(2,1)S(1)} %collective-permute-done.11.refs_1_), custom_call_target="tpu_custom_call" | custom-call | flops 234881024 | bytes 3211264 | tf_op jit(solution)/shard_map/pallas_call | solution.py:178
  135.5 3.3 %collective-permute-start.16 = (bf16[64,3712]{1,0:T(8,128)(2,1)S(1)}, bf16[64,3712]{1,0:T(8,128)(2,1)S(1)}, u32[]{:S(2)}, u32[]{:S(2)}) collective-permute-start(bf16[64,3712]{1,0:T(8,128)(2,1)S(1)} %slice.53), channel_id=1, source_target_pairs={{0,7},{1,0},{2,1},{3,2},{4,3},{5,4},{6,5},{7,6},{8,15},{9,8},{10,9... | collective-permute-start | bytes 1425416 | tf_op jit(solution)/shard_map/ppermute | solution.py:300
  142.2 6.3 %collective-permute-done.13 = bf16[2,24,3584]{2,1,0:T(8,128)(2,1)} collective-permute-done((bf16[2,24,3584]{2,1,0:T(8,128)(2,1)}, bf16[2,24,3584]{2,1,0:T(8,128)(2,1)}, u32[]{:S(2)}, u32[]{:S(2)}) %collective-permute-start.13) | collective-permute-done | bytes 344096 | tf_op jit(solution)/shard_map/ppermute | solution.py:300
  156.8 2.8 %collective-permute-done.17 = bf16[1,24,3584]{2,1,0:T(8,128)(2,1)S(1)} collective-permute-done((bf16[1,24,3584]{2,1,0:T(8,128)(2,1)S(1)}, bf16[1,24,3584]{2,1,0:T(8,128)(2,1)S(1)}, u32[]{:S(2)}, u32[]{:S(2)}) %collective-permute-start.17) | collective-permute-done | bytes 172064 | tf_op jit(solution)/shard_map/ppermute | solution.py:300
  159.6 3.1 %collective-permute-done.18 = bf16[1,24,3584]{2,1,0:T(8,128)(2,1)S(1)} collective-permute-done((bf16[1,24,3584]{2,1,0:T(8,128)(2,1)S(1)}, bf16[1,24,3584]{2,1,0:T(8,128)(2,1)S(1)}, u32[]{:S(2)}, u32[]{:S(2)}) %collective-permute-start.18) | collective-permute-done | bytes 172064 | tf_op jit(solution)/shard_map/ppermute | solution.py:300
  163.0 6.2 %convolution_convert_fusion = bf16[3584,1024]{1,0:T(8,128)(2,1)S(1)} fusion(bf16[768,1024]{1,0:T(8,128)(2,1)S(1)} %to_relative.1, bf16[288,3584]{1,0:T(8,128)(2,1)S(1)} %bitcast.59, bf16[480,3584]{1,0:T(8,128)(2,1)S(1)} %copy-done.13), kind=kOutput, calls=%fused_computation | convolution fusion | flops 5651824640 | bytes 14417920 | tf_op jit(solution)/shard_map/dot_general | solution.py:402
  169.2 2.3 dynamic-slice_bitcast_fusion
  173.4 2.3 convolution_convert_fusion.2
  177.6 7.3 %all-to-all-start = ((bf16[32,24,1024]{2,1,0:T(8,128)(2,1)}), bf16[32,24,1024]{2,1,0:T(8,128)(2,1)S(1)}, u32[]{:S(2)}, u32[]{:S(2)}) async-start(bf16[32,24,1024]{2,1,0:T(8,128)(2,1)} %bitcast.6), calls=%async_computation | async-start | bytes 3145728 | tf_op jit(solution)/shard_map/all_to_all | solution.py:332
  185.6 6.2 %pieces.1 = bf16[4,448,1024]{2,1,0:T(8,128)(2,1)} custom-call(s32[2]{0:T(128)} %pad_add_fusion.1.at_ref, bf16[4,2,448,1024]{3,2,1,0:T(8,128)(2,1)} %bitcast.56, bf16[4,448,1024]{2,1,0:T(8,128)(2,1)} %collective-permute-done.20.other_ref), custom_call_target="tpu_custom_call" | custom-call | flops 1835008 | bytes 11010048 | tf_op jit(solution)/shard_map/pieces/pallas_call | solution.py:92
  191.9 2.5 %slice_bitcast_fusion.3 = (bf16[448,512]{1,0:T(8,128)(2,1)}, bf16[448,512]{1,0:T(8,128)(2,1)S(1)}, bf16[448,512]{1,0:T(8,128)(2,1)}, bf16[448,512]{1,0:T(8,128)(2,1)S(1)}) fusion(bf16[4,448,1024]{2,1,0:T(8,128)(2,1)} %pieces.1), kind=kLoop, calls=%fused_computation.29 | loop fusion | bytes 3670016 | tf_op jit(solution)/shard_map/squeeze | solution.py:420
  196.4 2.4 %collective-permute-start.23 = (bf16[448,512]{1,0:T(8,128)(2,1)}, bf16[448,512]{1,0:T(8,128)(2,1)}, u32[]{:S(2)}, u32[]{:S(2)}) collective-permute-start(bf16[448,512]{1,0:T(8,128)(2,1)} %get-tuple-element.46), channel_id=1, source_target_pairs={{0,64},{64,128},{128,192},{192,0},{1,65},{65,129},{129,193},{193,1... | collective-permute-start | bytes 1376264 | tf_op jit(solution)/shard_map/ppermute | solution.py:300
  198.8 9.0 %collective-permute-done.25 = bf16[448,512]{1,0:T(8,128)(2,1)S(1)} collective-permute-done((bf16[448,512]{1,0:T(8,128)(2,1)S(1)}, bf16[448,512]{1,0:T(8,128)(2,1)S(1)}, u32[]{:S(2)}, u32[]{:S(2)}) %collective-permute-start.25) | collective-permute-done | bytes 458784 | tf_op jit(solution)/shard_map/ppermute | solution.py:300
  208.3 2.3 %fusion.11 = (bf16[448,512]{1,0:T(8,128)(2,1)}, bf16[448,512]{1,0:T(8,128)(2,1)}) fusion(bf16[448,512]{1,0:T(8,128)(2,1)S(1)} %collective-permute-done.25, bf16[4,448,1024]{2,1,0:T(8,128)(2,1)} %pieces.1, bf16[448,512]{1,0:T(8,128)(2,1)S(1)} %collective-permute-done.21), kind=kLoop, calls=%fused_computation.22 | loop fusion | flops 1835008 | bytes 2752512 | tf_op jit(solution)/shard_map/convert_element_type | solution.py:422
  213.6 3.1 %copy-done.1 = bf16[1,3584,1024]{2,1,0:T(8,128)(2,1)S(1)} copy-done((bf16[1,3584,1024]{2,1,0:T(8,128)(2,1)S(1)}, bf16[1,3584,1024]{2,1,0:T(8,128)(2,1)}, u32[]{:S(2)}) %copy-start.1) | copy-done | bytes 7340056
  217.8 7.0 %all-to-all-done = bf16[32,24,1024]{2,1,0:T(8,128)(2,1)S(1)} async-done(((bf16[32,24,1024]{2,1,0:T(8,128)(2,1)}), bf16[32,24,1024]{2,1,0:T(8,128)(2,1)S(1)}, u32[]{:S(2)}, u32[]{:S(2)}) %all-to-all-start) | async-done | bytes 1572896 | tf_op jit(solution)/shard_map/all_to_all | solution.py:332
  227.1 3.6 %fusion.6 = f32[1,448,1024]{2,1,0:T(8,128)} fusion(bf16[448,1024]{1,0:T(8,128)(2,1)S(1)} %kept.1, bf16[4,448,1024]{2,1,0:T(8,128)(2,1)} %pieces.1, bf16[448,512]{1,0:T(8,128)(2,1)} %collective-permute-done.23, bf16[448,512]{1,0:T(8,128)(2,1)} %collective-permute-done.22, bf16[448,512]{1,0:T(8,128)(2,1)} %collective-permute-done.26, ...), kind=kLoop, calls=%fused_computation.10 | loop fusion | flops 5963776 | bytes 5505024 | tf_op jit(solution)/shard_map/broadcast_in_dim | solution.py:429
  (106 shorter events, 51.1 us)
Async XLA Ops:
  3.5 35.4 %collective-permute-start = (bf16[128,3712]{1,0:T(8,128)(2,1)S(1)}, bf16[128,3712]{1,0:T(8,128)(2,1)}, u32[]{:S(2)}, u32[]{:S(2)}) collective-permute-start(bf16[128,3712]{1,0:T(8,128)(2,1)S(1)} %fusion.10.refs_0_), channel_id=1, source_target_pairs={{0,1},{1,2},{2,3},{3,4},{4,5},{5,6},{6,7},{7,0},{8,9},{9,10},{10,1... | collective-permute-start | bytes 2850824 | tf_op jit(solution)/shard_map/ppermute | solution.py:300
  5.5 33.4 %collective-permute-start.1 = (bf16[128,3712]{1,0:T(8,128)(2,1)S(1)}, bf16[128,3712]{1,0:T(8,128)(2,1)S(1)}, u32[]{:S(2)}, u32[]{:S(2)}) collective-permute-start(bf16[128,3712]{1,0:T(8,128)(2,1)S(1)} %fusion.10.refs_0_), channel_id=1, source_target_pairs={{0,7},{1,0},{2,1},{3,2},{4,3},{5,4},{6,5},{7,6},{8,15},{9,8},{10,9... | collective-permute-start | bytes 2850824 | tf_op jit(solution)/shard_map/ppermute | solution.py:300
  15.2 124.4 %all-to-all-start.1 = ((bf16[32,24,1024]{2,1,0:T(8,128)(2,1)}), bf16[32,24,1024]{2,1,0:T(8,128)(2,1)S(1)}, u32[]{:S(2)}, u32[]{:S(2)}) async-start(bf16[32,24,1024]{2,1,0:T(8,128)(2,1)} %bitcast.57), calls=%async_computation.1 | async-start | bytes 3145728 | tf_op jit(solution)/shard_map/all_to_all | solution.py:332
  38.9 45.7 %collective-permute-start.5 = (bf16[128,3712]{1,0:T(8,128)(2,1)}, bf16[128,3712]{1,0:T(8,128)(2,1)}, u32[]{:S(2)}, u32[]{:S(2)}) collective-permute-start(bf16[128,3712]{1,0:T(8,128)(2,1)} %collective-permute-done.refs_1_), channel_id=1, source_target_pairs={{0,1},{1,2},{2,3},{3,4},{4,5},{5,6},{6,7},{7,0},{8,9},{9,10},{10,1... | collective-permute-start | bytes 2850824 | tf_op jit(solution)/shard_map/ppermute | solution.py:300
  40.7 43.9 %collective-permute-start.6 = (bf16[128,3712]{1,0:T(8,128)(2,1)S(1)}, bf16[128,3712]{1,0:T(8,128)(2,1)}, u32[]{:S(2)}, u32[]{:S(2)}) collective-permute-start(bf16[128,3712]{1,0:T(8,128)(2,1)S(1)} %collective-permute-done.1.refs_2_), channel_id=1, source_target_pairs={{0,7},{1,0},{2,1},{3,2},{4,3},{5,4},{6,5},{7,6},{8,15},{9,8},{10,9... | collective-permute-start | bytes 2850824 | tf_op jit(solution)/shard_map/ppermute | solution.py:300
  46.3 46.2 %collective-permute-start.2 = (bf16[3,24,3584]{2,1,0:T(8,128)(2,1)S(1)}, bf16[3,24,3584]{2,1,0:T(8,128)(2,1)S(1)}, u32[]{:S(2)}, u32[]{:S(2)}) collective-permute-start(bf16[3,24,3584]{2,1,0:T(8,128)(2,1)S(1)} %get-tuple-element.26), channel_id=1, source_target_pairs={{0,8},{8,16},{16,24},{24,0},{1,9},{9,17},{17,25},{25,1},{2,10},{10... | collective-permute-start | bytes 1548296 | tf_op jit(solution)/shard_map/ppermute | solution.py:300
  48.1 46.0 %collective-permute-start.3 = (bf16[3,24,3584]{2,1,0:T(8,128)(2,1)S(1)}, bf16[3,24,3584]{2,1,0:T(8,128)(2,1)S(1)}, u32[]{:S(2)}, u32[]{:S(2)}) collective-permute-start(bf16[3,24,3584]{2,1,0:T(8,128)(2,1)S(1)} %get-tuple-element.27), channel_id=1, source_target_pairs={{0,16},{8,24},{16,0},{24,8},{1,17},{9,25},{17,1},{25,9},{2,18},{10... | collective-permute-start | bytes 1548296 | tf_op jit(solution)/shard_map/ppermute | solution.py:300
  50.8 46.2 %collective-permute-start.4 = (bf16[3,24,3584]{2,1,0:T(8,128)(2,1)S(1)}, bf16[3,24,3584]{2,1,0:T(8,128)(2,1)S(1)}, u32[]{:S(2)}, u32[]{:S(2)}) collective-permute-start(bf16[3,24,3584]{2,1,0:T(8,128)(2,1)S(1)} %get-tuple-element.28), channel_id=1, source_target_pairs={{0,24},{8,0},{16,8},{24,16},{1,25},{9,1},{17,9},{25,17},{2,26},{10... | collective-permute-start | bytes 1548296 | tf_op jit(solution)/shard_map/ppermute | solution.py:300
  84.7 41.9 %collective-permute-start.10 = (bf16[128,3712]{1,0:T(8,128)(2,1)}, bf16[128,3712]{1,0:T(8,128)(2,1)S(1)}, u32[]{:S(2)}, u32[]{:S(2)}) collective-permute-start(bf16[128,3712]{1,0:T(8,128)(2,1)} %collective-permute-done.5.refs_0_), channel_id=1, source_target_pairs={{0,1},{1,2},{2,3},{3,4},{4,5},{5,6},{6,7},{7,0},{8,9},{9,10},{10,1... | collective-permute-start | bytes 2850824 | tf_op jit(solution)/shard_map/ppermute | solution.py:300
  84.7 41.9 %collective-permute-start.11 = (bf16[128,3712]{1,0:T(8,128)(2,1)}, bf16[128,3712]{1,0:T(8,128)(2,1)S(1)}, u32[]{:S(2)}, u32[]{:S(2)}) collective-permute-start(bf16[128,3712]{1,0:T(8,128)(2,1)} %collective-permute-done.6.refs_1_), channel_id=1, source_target_pairs={{0,7},{1,0},{2,1},{3,2},{4,3},{5,4},{6,5},{7,6},{8,15},{9,8},{10,9... | collective-permute-start | bytes 2850824 | tf_op jit(solution)/shard_map/ppermute | solution.py:300
  92.5 11.3 %collective-permute-start.7 = (bf16[2,24,3584]{2,1,0:T(8,128)(2,1)}, bf16[2,24,3584]{2,1,0:T(8,128)(2,1)}, u32[]{:S(2)}, u32[]{:S(2)}) collective-permute-start(bf16[2,24,3584]{2,1,0:T(8,128)(2,1)} %get-tuple-element.30), channel_id=1, source_target_pairs={{0,8},{8,16},{16,24},{24,0},{1,9},{9,17},{17,25},{25,1},{2,10},{10... | collective-permute-start | bytes 1032200 | tf_op jit(solution)/shard_map/ppermute | solution.py:300
  94.1 17.2 %collective-permute-start.8 = (bf16[2,24,3584]{2,1,0:T(8,128)(2,1)}, bf16[2,24,3584]{2,1,0:T(8,128)(2,1)}, u32[]{:S(2)}, u32[]{:S(2)}) collective-permute-start(bf16[2,24,3584]{2,1,0:T(8,128)(2,1)} %get-tuple-element.31), channel_id=1, source_target_pairs={{0,16},{8,24},{16,0},{24,8},{1,17},{9,25},{17,1},{25,9},{2,18},{10... | collective-permute-start | bytes 1032200 | tf_op jit(solution)/shard_map/ppermute | solution.py:300
  97.8 13.5 %collective-permute-start.9 = (bf16[2,24,3584]{2,1,0:T(8,128)(2,1)}, bf16[2,24,3584]{2,1,0:T(8,128)(2,1)}, u32[]{:S(2)}, u32[]{:S(2)}) collective-permute-start(bf16[2,24,3584]{2,1,0:T(8,128)(2,1)} %get-tuple-element.32), channel_id=1, source_target_pairs={{0,24},{8,0},{16,8},{24,16},{1,25},{9,1},{17,9},{25,17},{2,26},{10... | collective-permute-start | bytes 1032200 | tf_op jit(solution)/shard_map/ppermute | solution.py:300
  129.5 10.8 %collective-permute-start.12 = (bf16[2,24,3584]{2,1,0:T(8,128)(2,1)}, bf16[2,24,3584]{2,1,0:T(8,128)(2,1)}, u32[]{:S(2)}, u32[]{:S(2)}) collective-permute-start(bf16[2,24,3584]{2,1,0:T(8,128)(2,1)} %get-tuple-element.36), channel_id=1, source_target_pairs={{0,8},{8,16},{16,24},{24,0},{1,9},{9,17},{17,25},{25,1},{2,10},{10... | collective-permute-start | bytes 1032200 | tf_op jit(solution)/shard_map/ppermute | solution.py:300
  131.4 17.2 %collective-permute-start.13 = (bf16[2,24,3584]{2,1,0:T(8,128)(2,1)}, bf16[2,24,3584]{2,1,0:T(8,128)(2,1)}, u32[]{:S(2)}, u32[]{:S(2)}) collective-permute-start(bf16[2,24,3584]{2,1,0:T(8,128)(2,1)} %get-tuple-element.37), channel_id=1, source_target_pairs={{0,16},{8,24},{16,0},{24,8},{1,17},{9,25},{17,1},{25,9},{2,18},{10... | collective-permute-start | bytes 1032200 | tf_op jit(solution)/shard_map/ppermute | solution.py:300
  133.1 16.5 %collective-permute-start.14 = (bf16[2,24,3584]{2,1,0:T(8,128)(2,1)}, bf16[2,24,3584]{2,1,0:T(8,128)(2,1)}, u32[]{:S(2)}, u32[]{:S(2)}) collective-permute-start(bf16[2,24,3584]{2,1,0:T(8,128)(2,1)} %get-tuple-element.38), channel_id=1, source_target_pairs={{0,24},{8,0},{16,8},{24,16},{1,25},{9,1},{17,9},{25,17},{2,26},{10... | collective-permute-start | bytes 1032200 | tf_op jit(solution)/shard_map/ppermute | solution.py:300
  135.5 15.1 %collective-permute-start.15 = (bf16[64,3712]{1,0:T(8,128)(2,1)}, bf16[64,3712]{1,0:T(8,128)(2,1)S(1)}, u32[]{:S(2)}, u32[]{:S(2)}) collective-permute-start(bf16[64,3712]{1,0:T(8,128)(2,1)} %slice.52), channel_id=1, source_target_pairs={{0,1},{1,2},{2,3},{3,4},{4,5},{5,6},{6,7},{7,0},{8,9},{9,10},{10,1... | collective-permute-start | bytes 1425416 | tf_op jit(solution)/shard_map/ppermute | solution.py:300
  135.5 15.1 %collective-permute-start.16 = (bf16[64,3712]{1,0:T(8,128)(2,1)S(1)}, bf16[64,3712]{1,0:T(8,128)(2,1)S(1)}, u32[]{:S(2)}, u32[]{:S(2)}) collective-permute-start(bf16[64,3712]{1,0:T(8,128)(2,1)S(1)} %slice.53), channel_id=1, source_target_pairs={{0,7},{1,0},{2,1},{3,2},{4,3},{5,4},{6,5},{7,6},{8,15},{9,8},{10,9... | collective-permute-start | bytes 1425416 | tf_op jit(solution)/shard_map/ppermute | solution.py:300
  140.2 22.7 %copy-start.13 = (bf16[480,3584]{1,0:T(8,128)(2,1)S(1)}, bf16[480,3584]{1,0:T(8,128)(2,1)}, u32[]{:S(2)}) copy-start(bf16[480,3584]{1,0:T(8,128)(2,1)} %get-tuple-element.43) | copy-start | bytes 10321924
  152.1 7.5 %collective-permute-start.17 = (bf16[1,24,3584]{2,1,0:T(8,128)(2,1)S(1)}, bf16[1,24,3584]{2,1,0:T(8,128)(2,1)S(1)}, u32[]{:S(2)}, u32[]{:S(2)}) collective-permute-start(bf16[1,24,3584]{2,1,0:T(8,128)(2,1)S(1)} %get-tuple-element.40), channel_id=1, source_target_pairs={{0,8},{8,16},{16,24},{24,0},{1,9},{9,17},{17,25},{25,1},{2,10},{10... | collective-permute-start | bytes 516104 | tf_op jit(solution)/shard_map/ppermute | solution.py:300
  152.8 9.8 %collective-permute-start.18 = (bf16[1,24,3584]{2,1,0:T(8,128)(2,1)S(1)}, bf16[1,24,3584]{2,1,0:T(8,128)(2,1)S(1)}, u32[]{:S(2)}, u32[]{:S(2)}) collective-permute-start(bf16[1,24,3584]{2,1,0:T(8,128)(2,1)S(1)} %get-tuple-element.41), channel_id=1, source_target_pairs={{0,16},{8,24},{16,0},{24,8},{1,17},{9,25},{17,1},{25,9},{2,18},{10... | collective-permute-start | bytes 516104 | tf_op jit(solution)/shard_map/ppermute | solution.py:300
  154.7 8.2 %collective-permute-start.19 = (bf16[1,24,3584]{2,1,0:T(8,128)(2,1)S(1)}, bf16[1,24,3584]{2,1,0:T(8,128)(2,1)S(1)}, u32[]{:S(2)}, u32[]{:S(2)}) collective-permute-start(bf16[1,24,3584]{2,1,0:T(8,128)(2,1)S(1)} %get-tuple-element.42), channel_id=1, source_target_pairs={{0,24},{8,0},{16,8},{24,16},{1,25},{9,1},{17,9},{25,17},{2,26},{10... | collective-permute-start | bytes 516104 | tf_op jit(solution)/shard_map/ppermute | solution.py:300
  159.6 13.8 %slice-start = ((s8[7340032]{0:T(1024)(128)(4,1)}), s8[4194304]{0:T(1024)(128)(4,1)S(1)}, s32[]{:S(2)}) async-start(s8[7340032]{0:T(1024)(128)(4,1)} %bitcast.50), calls=%async_computation.2 | async-start | bytes 8388608
  162.9 10.5 %slice-start.1 = ((s8[7340032]{0:T(1024)(128)(4,1)}), s8[3145728]{0:T(1024)(128)(4,1)S(1)}, s32[]{:S(2)}) async-start(s8[7340032]{0:T(1024)(128)(4,1)} %bitcast.50), calls=%async_computation.3 | async-start | bytes 6291456
  173.3 12.3 %collective-permute-start.20 = (bf16[4,448,1024]{2,1,0:T(8,128)(2,1)}, bf16[4,448,1024]{2,1,0:T(8,128)(2,1)}, u32[]{:S(2)}, u32[]{:S(2)}) collective-permute-start(bf16[4,448,1024]{2,1,0:T(8,128)(2,1)} %dynamic-slice_bitcast_fusion), channel_id=1, source_target_pairs={{0,32},{32,0},{1,33},{33,1},{2,34},{34,2},{3,35},{35,3},{4,36},{36... | collective-permute-start | bytes 11010056 | tf_op jit(solution)/shard_map/ppermute | solution.py:300
  177.6 47.2 %all-to-all-start = ((bf16[32,24,1024]{2,1,0:T(8,128)(2,1)}), bf16[32,24,1024]{2,1,0:T(8,128)(2,1)S(1)}, u32[]{:S(2)}, u32[]{:S(2)}) async-start(bf16[32,24,1024]{2,1,0:T(8,128)(2,1)} %bitcast.6), calls=%async_computation | async-start | bytes 3145728 | tf_op jit(solution)/shard_map/all_to_all | solution.py:332
  194.4 13.4 %collective-permute-start.25 = (bf16[448,512]{1,0:T(8,128)(2,1)S(1)}, bf16[448,512]{1,0:T(8,128)(2,1)S(1)}, u32[]{:S(2)}, u32[]{:S(2)}) collective-permute-start(bf16[448,512]{1,0:T(8,128)(2,1)S(1)} %get-tuple-element.45), channel_id=1, source_target_pairs={{0,192},{64,0},{128,64},{192,128},{1,193},{65,1},{129,65},{193,129... | collective-permute-start | bytes 1376264 | tf_op jit(solution)/shard_map/ppermute | solution.py:300
  194.9 13.4 %collective-permute-start.21 = (bf16[448,512]{1,0:T(8,128)(2,1)S(1)}, bf16[448,512]{1,0:T(8,128)(2,1)S(1)}, u32[]{:S(2)}, u32[]{:S(2)}) collective-permute-start(bf16[448,512]{1,0:T(8,128)(2,1)S(1)} %get-tuple-element.47), channel_id=1, source_target_pairs={{0,64},{64,128},{128,192},{192,0},{1,65},{65,129},{129,193},{193,1... | collective-permute-start | bytes 1376264 | tf_op jit(solution)/shard_map/ppermute | solution.py:300
  196.4 30.7 %collective-permute-start.23 = (bf16[448,512]{1,0:T(8,128)(2,1)}, bf16[448,512]{1,0:T(8,128)(2,1)}, u32[]{:S(2)}, u32[]{:S(2)}) collective-permute-start(bf16[448,512]{1,0:T(8,128)(2,1)} %get-tuple-element.46), channel_id=1, source_target_pairs={{0,64},{64,128},{128,192},{192,0},{1,65},{65,129},{129,193},{193,1... | collective-permute-start | bytes 1376264 | tf_op jit(solution)/shard_map/ppermute | solution.py:300
  198.8 28.3 %collective-permute-start.24 = (bf16[448,512]{1,0:T(8,128)(2,1)}, bf16[448,512]{1,0:T(8,128)(2,1)}, u32[]{:S(2)}, u32[]{:S(2)}) collective-permute-start(bf16[448,512]{1,0:T(8,128)(2,1)} %get-tuple-element.44), channel_id=1, source_target_pairs={{0,192},{64,0},{128,64},{192,128},{1,193},{65,1},{129,65},{193,129... | collective-permute-start | bytes 1376264 | tf_op jit(solution)/shard_map/ppermute | solution.py:300
  210.6 16.5 %collective-permute-start.22 = (bf16[448,512]{1,0:T(8,128)(2,1)}, bf16[448,512]{1,0:T(8,128)(2,1)}, u32[]{:S(2)}, u32[]{:S(2)}) collective-permute-start(bf16[448,512]{1,0:T(8,128)(2,1)} %get-tuple-element.49), channel_id=1, source_target_pairs={{0,64},{64,128},{128,192},{192,0},{1,65},{65,129},{129,193},{193,1... | collective-permute-start | bytes 1376264 | tf_op jit(solution)/shard_map/ppermute | solution.py:300
  212.5 14.6 %collective-permute-start.26 = (bf16[448,512]{1,0:T(8,128)(2,1)}, bf16[448,512]{1,0:T(8,128)(2,1)}, u32[]{:S(2)}, u32[]{:S(2)}) collective-permute-start(bf16[448,512]{1,0:T(8,128)(2,1)} %get-tuple-element.48), channel_id=1, source_target_pairs={{0,192},{64,0},{128,64},{192,128},{1,193},{65,1},{129,65},{193,129... | collective-permute-start | bytes 1376264 | tf_op jit(solution)/shard_map/ppermute | solution.py:300
  (13 other events, 39.6 us)
where the time goes:
time: 235 us; the launch traced here: 231 us
  waiting for transfers between devices  73.5 us (31%)
  starting transfers between devices  60 us (26%)
  Pallas kernels  44.6 us (19%)
  local copies, waits for them, and re-layouts  28.9 us (12%)
  matrix products  13.2 us (6%)
  other arithmetic  9.39 us (4%)
    ppermute x27, waiting for transfers between devices, shift(): return lax.ppermute(a, axis, [(i, (i + by) % size) for i in range(size)])  66.5 us
    ppermute x27, starting transfers between devices, shift(): return lax.ppermute(a, axis, [(i, (i + by) % size) for i in range(size)])  43.9 us
    unnamed x40, local copies, waits for them, and re-layouts  19.7 us
    all_to_all x2, starting transfers between devices, exchange(): lax.all_to_all(a.reshape(experts, cap, a.shape[-1]), ('y', 'z'), split_ax...  16.1 us
    pallas_call x1, Pallas kernels, multiply(): pl.pallas_call(multiply_kernel, out_shape=[jax.ShapeDtypeStruct((rows, hi...  15.3 us
    pallas_call x4, Pallas kernels, pick(): pl.pallas_call(functools.partial(pick_kernel, ny, nz, cap, topk, feat, sh...  11.5 us
    pallas_call x1, Pallas kernels, dequantize(): pl.pallas_call(dequantize_kernel, out_shape=jax.ShapeDtypeStruct((feat, h...  8.07 us
    all_to_all x2, waiting for transfers between devices, exchange(): lax.all_to_all(a.reshape(experts, cap, a.shape[-1]), ('y', 'z'), split_ax...  7.03 us
  transfers between devices with their start and end apart: 29, of which 10 were waited for; matrix products, arithmetic and copies ran while one was open for 9% of the time, Pallas kernels for 19%

commit v1 on v0

--- a/solution.py
+++ b/solution.py
@@ -30,7 +30,7 @@
 
 def dequantize(weight_one, exponent_one):
     feat, hidden = weight_one.shape
-    step = 256
+    step = 128
     return pl.pallas_call(
         dequantize_kernel,
         out_shape=jax.ShapeDtypeStruct((feat, hidden), jnp.bfloat16),
@@ -220,7 +220,7 @@
 
 def multiply(pieces, weight):
     cap, feat = pieces[0].shape[1:]
-    rows, hidden, step = sum(p.shape[0] for p in pieces) * cap, weight.shape[1], 256
+    rows, hidden, step = sum(p.shape[0] for p in pieces) * cap, weight.shape[1], 512
     return pl.pallas_call(
         multiply_kernel,
         out_shape=[
@@ -360,7 +360,7 @@
 
     def finish(name, *groups):
         group_pieces = [p for g in groups for p in got[g]]
-        if name == 0:
+        if name < 2:
             back, here = multiply(group_pieces, quantized)
         else:
             here = jnp.concatenate(group_pieces, axis=0).reshape(-1, feat)
@@ -388,10 +388,12 @@
     right, left = hop(right[: tok // 2], left[tok // 2 :])
     got_inputs = exchange(send_inputs)
     deliver((right, left))
-    finish(0, 0, 1)
-    finish(1, 2, 3)
+    finish(0, 0)
+    finish(1, 1, 2)
+    finish(2, 3)
 
     back = to_absolute(at, backs, ny, nz, cap)
+    back, got_inputs = lax.optimization_barrier((back, got_inputs))
     returned = exchange(back).reshape(rows, hidden)
     input_grads = jnp.dot(place.T, returned, preferred_element_type=jnp.float32).astype(
         jnp.bfloat16

time: 235 us -> 239 us (1.017); the launches traced: 231 us -> 237 us
  Pallas kernels: 44.6 us -> 49.8 us
  matrix products: 13.2 us -> 16.7 us
  waiting for transfers between devices: 73.5 us -> 76.1 us
  starting transfers between devices: 60 us -> 57.6 us
    unnamed x40 -> x41, local copies, waits for them, and re-layouts: 19.7 us -> 15.1 us
    pallas_call x1 -> x2, Pallas kernels: 15.3 us -> 19.2 us  [multiply(): pl.pallas_call(multiply_kernel, out_shape=[jax.ShapeDtypeStruct((rows, hi...]
    ppermute x27, waiting for transfers between devices: 66.5 us -> 69.6 us  [shift(): return lax.ppermute(a, axis, [(i, (i + by) % size) for i in range(size)])]
  transfers between devices with their start and end apart: 29 -> 29, of which waited for: 10 -> 13; matrix products, arithmetic and copies ran while one was open for 9% -> 9% of each run, Pallas kernels for 19% -> 21%
where the time goes in v1:
time: 239 us; the launch traced here: 237 us
  waiting for transfers between devices  76.1 us (32%)
  starting transfers between devices  57.6 us (24%)
  Pallas kernels  49.8 us (21%)
  local copies, waits for them, and re-layouts  26.7 us (11%)
  matrix products  16.7 us (7%)
  other arithmetic  9.28 us (4%)
    ppermute x27, waiting for transfers between devices, shift(): return lax.ppermute(a, axis, [(i, (i + by) % size) for i in range(size)])  69.6 us
    ppermute x27, starting transfers between devices, shift(): return lax.ppermute(a, axis, [(i, (i + by) % size) for i in range(size)])  42 us
    pallas_call x2, Pallas kernels, multiply(): pl.pallas_call(multiply_kernel, out_shape=[jax.ShapeDtypeStruct((rows, hi...  19.2 us
    all_to_all x2, starting transfers between devices, exchange(): lax.all_to_all(a.reshape(experts, cap, a.shape[-1]), ('y', 'z'), split_ax...  15.6 us
    unnamed x41, local copies, waits for them, and re-layouts  15.1 us
    pallas_call x4, Pallas kernels, pick(): pl.pallas_call(functools.partial(pick_kernel, ny, nz, cap, topk, feat, sh...  11.2 us
    pallas_call x1, Pallas kernels, dequantize(): pl.pallas_call(dequantize_kernel, out_shape=jax.ShapeDtypeStruct((feat, h...  9.53 us
    dot_general x1, matrix products, local(): lax.dot_general(all_grads, to_relative(at, got_inputs, ny, nz, cap), (((0...  7.55 us
  transfers between devices with their start and end apart: 29, of which 13 were waited for; matrix products, arithmetic and copies ran while one was open for 9% of the time, Pallas kernels for 21%

profile of v1, /device:TPU:4, one launch (start us, length us, event | category | flops | bytes accessed | tf_op | source)
XLA Modules:
  0.0 237.1 jit_solution(11976932183966761453)
XLA Ops:
  5.4 4.0 %collective-permute-start.1 = (bf16[128,3712]{1,0:T(8,128)(2,1)S(1)}, bf16[128,3712]{1,0:T(8,128)(2,1)}, u32[]{:S(2)}, u32[]{:S(2)}) collective-permute-start(bf16[128,3712]{1,0:T(8,128)(2,1)S(1)} %fusion.12.refs_0_), channel_id=1, source_target_pairs={{0,7},{1,0},{2,1},{3,2},{4,3},{5,4},{6,5},{7,6},{8,15},{9,8},{10,9... | collective-permute-start | bytes 2850824 | tf_op jit(solution)/shard_map/ppermute | solution.py:300
  9.5 3.1 %copy-done.1 = bf16[1,3584,1024]{2,1,0:T(8,128)(2,1)S(1)} copy-done((bf16[1,3584,1024]{2,1,0:T(8,128)(2,1)S(1)}, bf16[1,3584,1024]{2,1,0:T(8,128)(2,1)}, u32[]{:S(2)}) %copy-start.1) | copy-done | bytes 7340056
  12.6 9.5 %dequantize.1.refs_4_.refs_8_ = bf16[3584,1024]{1,0:T(8,128)(2,1)S(1)} custom-call(bf16[3584,1024]{1,0:T(8,128)(2,1)S(1)} %bitcast.48, s32[8,3584]{1,0:T(8,128)S(1)} %bitcast.52), custom_call_target="tpu_custom_call" | custom-call | flops 44040192 | bytes 14680064 | tf_op jit(solution)/shard_map/dequantize/pallas_call | solution.py:34
  22.1 2.9 %copy-done = bf16[3584,1024]{1,0:T(8,128)(2,1)} copy-done((bf16[3584,1024]{1,0:T(8,128)(2,1)}, bf16[3584,1024]{1,0:T(8,128)(2,1)S(1)}, u32[]{:S(2)}) %copy-start) | copy-done | bytes 7340056
  25.0 5.4 %collective-permute-done.refs_1_ = bf16[128,3712]{1,0:T(8,128)(2,1)S(1)} collective-permute-done((bf16[128,3712]{1,0:T(8,128)(2,1)S(1)}, bf16[128,3712]{1,0:T(8,128)(2,1)S(1)}, u32[]{:S(2)}, u32[]{:S(2)}) %collective-permute-start) | collective-permute-done | bytes 950304 | tf_op jit(solution)/shard_map/ppermute | solution.py:300
  30.4 3.2 %collective-permute-start.6 = (bf16[128,3712]{1,0:T(8,128)(2,1)}, bf16[128,3712]{1,0:T(8,128)(2,1)}, u32[]{:S(2)}, u32[]{:S(2)}) collective-permute-start(bf16[128,3712]{1,0:T(8,128)(2,1)} %collective-permute-done.1.refs_2_), channel_id=1, source_target_pairs={{0,7},{1,0},{2,1},{3,2},{4,3},{5,4},{6,5},{7,6},{8,15},{9,8},{10,9... | collective-permute-start | bytes 2850824 | tf_op jit(solution)/shard_map/ppermute | solution.py:300
  35.3 3.4 %convolution_convert_fusion.1 = bf16[768,1024]{1,0:T(8,128)(2,1)} fusion(bf16[512,1024]{1,0:T(8,128)(2,1)} %reshape.50, s32[512]{0:T(512)S(1)} %convert_add_fusion.3), kind=kOutput, calls=%fused_computation.13 | convolution fusion | flops 806486016 | bytes 2623488 | tf_op jit(solution)/shard_map/dot_general | solution.py:336
  38.7 8.6 %all-to-all-start = ((bf16[32,24,1024]{2,1,0:T(8,128)(2,1)}), bf16[32,24,1024]{2,1,0:T(8,128)(2,1)S(1)}, u32[]{:S(2)}, u32[]{:S(2)}) async-start(bf16[32,24,1024]{2,1,0:T(8,128)(2,1)} %bitcast.57), calls=%async_computation | async-start | bytes 3145728 | tf_op jit(solution)/shard_map/all_to_all | solution.py:332
  47.2 10.5 %collective-permute-done.5.refs_0_ = bf16[128,3712]{1,0:T(8,128)(2,1)} collective-permute-done((bf16[128,3712]{1,0:T(8,128)(2,1)S(1)}, bf16[128,3712]{1,0:T(8,128)(2,1)}, u32[]{:S(2)}, u32[]{:S(2)}) %collective-permute-start.5) | collective-permute-done | bytes 950304 | tf_op jit(solution)/shard_map/ppermute | solution.py:300
  61.2 4.4 %collective-permute-start.11 = (bf16[128,3712]{1,0:T(8,128)(2,1)}, bf16[128,3712]{1,0:T(8,128)(2,1)}, u32[]{:S(2)}, u32[]{:S(2)}) collective-permute-start(bf16[128,3712]{1,0:T(8,128)(2,1)} %collective-permute-done.6.refs_1_), channel_id=1, source_target_pairs={{0,7},{1,0},{2,1},{3,2},{4,3},{5,4},{6,5},{7,6},{8,15},{9,8},{10,9... | collective-permute-start | bytes 2850824 | tf_op jit(solution)/shard_map/ppermute | solution.py:300
  66.9 3.3 %shard_map.77 = (bf16[3,24,3584]{2,1,0:T(8,128)(2,1)S(1)}, bf16[3,24,3584]{2,1,0:T(8,128)(2,1)S(1)}, bf16[3,24,3584]{2,1,0:T(8,128)(2,1)S(1)}, bf16[3,24,3584]{2,1,0:T(8,128)(2,1)S(1)}) custom-call(s32[2]{0:T(128)S(1)} %pad_add_fusion.at_ref, bf16[128,3712]{1,0:T(8,128)(2,1)S(1)} %fusion.12.refs_0_, bf16[128,3712]{1,0:T(8,128)(2,1)S(1)} %copy-done.4, ...), custom_call_target="tpu_custom_call" | custom-call | flops 352321536 | bytes 4816896 | tf_op jit(solution)/shard_map/pallas_call | solution.py:178
  72.5 2.9 %collective-permute-start.3 = (bf16[3,24,3584]{2,1,0:T(8,128)(2,1)S(1)}, bf16[3,24,3584]{2,1,0:T(8,128)(2,1)S(1)}, u32[]{:S(2)}, u32[]{:S(2)}) collective-permute-start(bf16[3,24,3584]{2,1,0:T(8,128)(2,1)S(1)} %get-tuple-element.31), channel_id=1, source_target_pairs={{0,16},{8,24},{16,0},{24,8},{1,17},{9,25},{17,1},{25,9},{2,18},{10... | collective-permute-start | bytes 1548296 | tf_op jit(solution)/shard_map/ppermute | solution.py:300
  76.8 2.9 %shard_map.78 = (bf16[2,24,3584]{2,1,0:T(8,128)(2,1)S(1)}, bf16[2,24,3584]{2,1,0:T(8,128)(2,1)S(1)}, bf16[2,24,3584]{2,1,0:T(8,128)(2,1)S(1)}, bf16[2,24,3584]{2,1,0:T(8,128)(2,1)S(1)}) custom-call(s32[2]{0:T(128)S(1)} %pad_add_fusion.at_ref, bf16[128,3712]{1,0:T(8,128)(2,1)} %collective-permute-done.5.refs_0_, bf16[128,3712]{1,0:T(8,128)(2,1)} %collective-permute-done.6.refs_1_), custom_call_target="tpu_custom_call" | custom-call | flops 234881024 | bytes 3211264 | tf_op jit(solution)/shard_map/pallas_call | solution.py:178
  80.4 18.9 %collective-permute-done.2.refs_1_ = bf16[3,24,3584]{2,1,0:T(8,128)(2,1)S(1)} collective-permute-done((bf16[3,24,3584]{2,1,0:T(8,128)(2,1)S(1)}, bf16[3,24,3584]{2,1,0:T(8,128)(2,1)S(1)}, u32[]{:S(2)}, u32[]{:S(2)}) %collective-permute-start.2) | collective-permute-done | bytes 516128 | tf_op jit(solution)/shard_map/ppermute | solution.py:300
  99.3 8.6 %collective-permute-done.10.refs_0_ = bf16[128,3712]{1,0:T(8,128)(2,1)S(1)} collective-permute-done((bf16[128,3712]{1,0:T(8,128)(2,1)}, bf16[128,3712]{1,0:T(8,128)(2,1)S(1)}, u32[]{:S(2)}, u32[]{:S(2)}) %collective-permute-start.10) | collective-permute-done | bytes 950304 | tf_op jit(solution)/shard_map/ppermute | solution.py:300
  107.9 3.2 %collective-permute-start.8 = (bf16[2,24,3584]{2,1,0:T(8,128)(2,1)S(1)}, bf16[2,24,3584]{2,1,0:T(8,128)(2,1)S(1)}, u32[]{:S(2)}, u32[]{:S(2)}) collective-permute-start(bf16[2,24,3584]{2,1,0:T(8,128)(2,1)S(1)} %get-tuple-element.37), channel_id=1, source_target_pairs={{0,16},{8,24},{16,0},{24,8},{1,17},{9,25},{17,1},{25,9},{2,18},{10... | collective-permute-start | bytes 1032200 | tf_op jit(solution)/shard_map/ppermute | solution.py:300
  112.2 3.6 %shard_map.79 = (bf16[2,24,3584]{2,1,0:T(8,128)(2,1)S(1)}, bf16[2,24,3584]{2,1,0:T(8,128)(2,1)}, bf16[2,24,3584]{2,1,0:T(8,128)(2,1)}, bf16[2,24,3584]{2,1,0:T(8,128)(2,1)}) custom-call(s32[2]{0:T(128)S(1)} %pad_add_fusion.at_ref, bf16[128,3712]{1,0:T(8,128)(2,1)S(1)} %collective-permute-done.10.refs_0_, bf16[128,3712]{1,0:T(8,128)(2,1)} %collective-permute-done.11.refs_1_), custom_call_target="tpu_custom_call" | custom-call | flops 234881024 | bytes 3211264 | tf_op jit(solution)/shard_map/pallas_call | solution.py:178
  117.7 2.5 %collective-permute-start.14 = (bf16[2,24,3584]{2,1,0:T(8,128)(2,1)}, bf16[2,24,3584]{2,1,0:T(8,128)(2,1)}, u32[]{:S(2)}, u32[]{:S(2)}) collective-permute-start(bf16[2,24,3584]{2,1,0:T(8,128)(2,1)} %get-tuple-element.42), channel_id=1, source_target_pairs={{0,24},{8,0},{16,8},{24,16},{1,25},{9,1},{17,9},{25,17},{2,26},{10... | collective-permute-start | bytes 1032200 | tf_op jit(solution)/shard_map/ppermute | solution.py:300
  122.3 5.8 %collective-permute-done.9.refs_3_ = bf16[2,24,3584]{2,1,0:T(8,128)(2,1)S(1)} collective-permute-done((bf16[2,24,3584]{2,1,0:T(8,128)(2,1)S(1)}, bf16[2,24,3584]{2,1,0:T(8,128)(2,1)S(1)}, u32[]{:S(2)}, u32[]{:S(2)}) %collective-permute-start.9) | collective-permute-done | bytes 344096 | tf_op jit(solution)/shard_map/ppermute | solution.py:300
  130.5 9.1 %multiply.2 = (bf16[288,1024]{1,0:T(8,128)(2,1)}, bf16[288,3584]{1,0:T(8,128)(2,1)}) custom-call(bf16[3,24,3584]{2,1,0:T(8,128)(2,1)} %copy-done.6, bf16[3,24,3584]{2,1,0:T(8,128)(2,1)} %copy-done.12, bf16[3,24,3584]{2,1,0:T(8,128)(2,1)} %copy-done.13, bf16[3,24,3584]{2,1,0:T(8,128)(2,1)} %copy-done.14, bf16[3584,1024]{1,0:T(8,128)(2,1)} %copy-done), custom_call_target="tpu_custom_call" | custom-call | flops 2113929216 | bytes 9404416 | tf_op jit(solution)/shard_map/multiply/pallas_call | solution.py:224
  140.5 10.1 %multiply.3 = (bf16[384,1024]{1,0:T(8,128)(2,1)}, bf16[384,3584]{1,0:T(8,128)(2,1)}) custom-call(bf16[2,24,3584]{2,1,0:T(8,128)(2,1)} %copy-done.8, bf16[2,24,3584]{2,1,0:T(8,128)(2,1)} %copy-done.17, bf16[2,24,3584]{2,1,0:T(8,128)(2,1)} %copy-done.18, bf16[2,24,3584]{2,1,0:T(8,128)(2,1)} %copy-done.19, bf16[2,24,3584]{2,1,0:T(8,128)(2,1)} %copy-done.9, ...), custom_call_target="tpu_custom_call" | custom-call | flops 2818572288 | bytes 10092544 | tf_op jit(solution)/shard_map/multiply/pallas_call | solution.py:224
  153.3 2.9 %collective-permute-start.18 = (bf16[1,24,3584]{2,1,0:T(8,128)(2,1)S(1)}, bf16[1,24,3584]{2,1,0:T(8,128)(2,1)S(1)}, u32[]{:S(2)}, u32[]{:S(2)}) collective-permute-start(bf16[1,24,3584]{2,1,0:T(8,128)(2,1)S(1)} %get-tuple-element.46), channel_id=1, source_target_pairs={{0,16},{8,24},{16,0},{24,8},{1,17},{9,25},{17,1},{25,9},{2,18},{10... | collective-permute-start | bytes 516104 | tf_op jit(solution)/shard_map/ppermute | solution.py:300
  159.3 4.9 %collective-permute-done.18 = bf16[1,24,3584]{2,1,0:T(8,128)(2,1)S(1)} collective-permute-done((bf16[1,24,3584]{2,1,0:T(8,128)(2,1)S(1)}, bf16[1,24,3584]{2,1,0:T(8,128)(2,1)S(1)}, u32[]{:S(2)}, u32[]{:S(2)}) %collective-permute-start.18) | collective-permute-done | bytes 172064 | tf_op jit(solution)/shard_map/ppermute | solution.py:300
  164.2 4.5 %convolution_convert_fusion.2.refs_3_ = bf16[96,1024]{1,0:T(8,128)(2,1)S(1)} fusion(bf16[96,3584]{1,0:T(8,128)(2,1)S(1)} %bitcast.55, bf16[3584,1024]{1,0:T(8,128)(2,1)} %copy-done), kind=kOutput, calls=%fused_computation.17 | convolution fusion | flops 704741376 | bytes 8224768 | tf_op jit(solution)/shard_map/dot_general | solution.py:367
  172.2 7.5 %convolution_convert_fusion = bf16[3584,1024]{1,0:T(8,128)(2,1)S(1)} fusion(bf16[768,1024]{1,0:T(8,128)(2,1)S(1)} %to_relative.1, bf16[96,3584]{1,0:T(8,128)(2,1)S(1)} %bitcast.56, bf16[384,3584]{1,0:T(8,128)(2,1)} %get-tuple-element.50, bf16[288,3584]{1,0:T(8,128)(2,1)S(1)} %copy-done.16), kind=kOutput, calls=%fused_computation | convolution fusion | flops 5657329664 | bytes 14417920 | tf_op jit(solution)/shard_map/dot_general | solution.py:404
  179.7 2.6 %dynamic-slice_bitcast_fusion = bf16[4,448,1024]{2,1,0:T(8,128)(2,1)} fusion(bf16[4,2,448,1024]{3,2,1,0:T(8,128)(2,1)S(1)} %bitcast.53, s32[]{:T(128)S(6)} %select_n.12), kind=kLoop, calls=%fused_computation.6 | loop fusion | bytes 7340036 | tf_op jit(solution)/shard_map/jit(dynamic_index_in_dim)/squeeze | solution.py:411
  183.9 7.0 %all-to-all-start.1 = ((bf16[32,24,1024]{2,1,0:T(8,128)(2,1)}), bf16[32,24,1024]{2,1,0:T(8,128)(2,1)S(1)}, u32[]{:S(2)}, u32[]{:S(2)}) async-start(bf16[32,24,1024]{2,1,0:T(8,128)(2,1)} %bitcast.7), calls=%async_computation.1 | async-start | bytes 3145728 | tf_op jit(solution)/shard_map/all_to_all | solution.py:332
  191.4 6.2 %pieces.1 = bf16[4,448,1024]{2,1,0:T(8,128)(2,1)} custom-call(s32[2]{0:T(128)} %pad_add_fusion.1.at_ref, bf16[4,2,448,1024]{3,2,1,0:T(8,128)(2,1)} %bitcast.54, bf16[4,448,1024]{2,1,0:T(8,128)(2,1)} %collective-permute-done.20.other_ref), custom_call_target="tpu_custom_call" | custom-call | flops 1835008 | bytes 11010048 | tf_op jit(solution)/shard_map/pieces/pallas_call | solution.py:92
  204.2 9.3 %collective-permute-done.21 = bf16[448,512]{1,0:T(8,128)(2,1)S(1)} collective-permute-done((bf16[448,512]{1,0:T(8,128)(2,1)S(1)}, bf16[448,512]{1,0:T(8,128)(2,1)S(1)}, u32[]{:S(2)}, u32[]{:S(2)}) %collective-permute-start.21) | collective-permute-done | bytes 458784 | tf_op jit(solution)/shard_map/ppermute | solution.py:300
  220.1 3.1 %copy-done.2 = bf16[1,3584,1024]{2,1,0:T(8,128)(2,1)S(1)} copy-done((bf16[1,3584,1024]{2,1,0:T(8,128)(2,1)S(1)}, bf16[1,3584,1024]{2,1,0:T(8,128)(2,1)}, u32[]{:S(2)}) %copy-start.2) | copy-done | bytes 7340056
  224.3 6.5 %all-to-all-done.1 = bf16[32,24,1024]{2,1,0:T(8,128)(2,1)S(1)} async-done(((bf16[32,24,1024]{2,1,0:T(8,128)(2,1)}), bf16[32,24,1024]{2,1,0:T(8,128)(2,1)S(1)}, u32[]{:S(2)}, u32[]{:S(2)}) %all-to-all-start.1) | async-done | bytes 1572896 | tf_op jit(solution)/shard_map/all_to_all | solution.py:332
  233.5 3.6 %fusion.8 = f32[1,448,1024]{2,1,0:T(8,128)} fusion(bf16[448,1024]{1,0:T(8,128)(2,1)S(1)} %kept.1, bf16[4,448,1024]{2,1,0:T(8,128)(2,1)} %pieces.1, bf16[448,512]{1,0:T(8,128)(2,1)} %collective-permute-done.23, bf16[448,512]{1,0:T(8,128)(2,1)} %collective-permute-done.22, bf16[448,512]{1,0:T(8,128)(2,1)} %collective-permute-done.26, ...), kind=kLoop, calls=%fused_computation.12 | loop fusion | flops 5963776 | bytes 5505024 | tf_op jit(solution)/shard_map/broadcast_in_dim | solution.py:431
  (104 shorter events, 52.2 us)
Async XLA Ops:
  3.4 27.0 %collective-permute-start = (bf16[128,3712]{1,0:T(8,128)(2,1)S(1)}, bf16[128,3712]{1,0:T(8,128)(2,1)S(1)}, u32[]{:S(2)}, u32[]{:S(2)}) collective-permute-start(bf16[128,3712]{1,0:T(8,128)(2,1)S(1)} %fusion.12.refs_0_), channel_id=1, source_target_pairs={{0,1},{1,2},{2,3},{3,4},{4,5},{5,6},{6,7},{7,0},{8,9},{9,10},{10,1... | collective-permute-start | bytes 2850824 | tf_op jit(solution)/shard_map/ppermute | solution.py:300
  5.4 25.0 %collective-permute-start.1 = (bf16[128,3712]{1,0:T(8,128)(2,1)S(1)}, bf16[128,3712]{1,0:T(8,128)(2,1)}, u32[]{:S(2)}, u32[]{:S(2)}) collective-permute-start(bf16[128,3712]{1,0:T(8,128)(2,1)S(1)} %fusion.12.refs_0_), channel_id=1, source_target_pairs={{0,7},{1,0},{2,1},{3,2},{4,3},{5,4},{6,5},{7,6},{8,15},{9,8},{10,9... | collective-permute-start | bytes 2850824 | tf_op jit(solution)/shard_map/ppermute | solution.py:300
  12.5 21.1 %copy-start.15 = (s32[128,4]{0,1:T(4,128)S(1)}, s32[128,4]{0,1:T(4,128)}, u32[]{:S(2)}) copy-start(s32[128,4]{0,1:T(4,128)} %param.8) | copy-start | bytes 6148
  12.6 21.3 %copy-start.11 = (bf16[128,4,1024]{2,1,0:T(4,128)(2,1)S(1)}, bf16[128,4,1024]{2,1,0:T(4,128)(2,1)}, u32[]{:S(2)}) copy-start(bf16[128,4,1024]{2,1,0:T(4,128)(2,1)} %param.9) | copy-start | bytes 3145732
  30.4 27.3 %collective-permute-start.5 = (bf16[128,3712]{1,0:T(8,128)(2,1)S(1)}, bf16[128,3712]{1,0:T(8,128)(2,1)}, u32[]{:S(2)}, u32[]{:S(2)}) collective-permute-start(bf16[128,3712]{1,0:T(8,128)(2,1)S(1)} %collective-permute-done.refs_1_), channel_id=1, source_target_pairs={{0,1},{1,2},{2,3},{3,4},{4,5},{5,6},{6,7},{7,0},{8,9},{9,10},{10,1... | collective-permute-start | bytes 2850824 | tf_op jit(solution)/shard_map/ppermute | solution.py:300
  30.4 30.8 %collective-permute-start.6 = (bf16[128,3712]{1,0:T(8,128)(2,1)}, bf16[128,3712]{1,0:T(8,128)(2,1)}, u32[]{:S(2)}, u32[]{:S(2)}) collective-permute-start(bf16[128,3712]{1,0:T(8,128)(2,1)} %collective-permute-done.1.refs_2_), channel_id=1, source_target_pairs={{0,7},{1,0},{2,1},{3,2},{4,3},{5,4},{6,5},{7,6},{8,15},{9,8},{10,9... | collective-permute-start | bytes 2850824 | tf_op jit(solution)/shard_map/ppermute | solution.py:300
  38.7 131.9 %all-to-all-start = ((bf16[32,24,1024]{2,1,0:T(8,128)(2,1)}), bf16[32,24,1024]{2,1,0:T(8,128)(2,1)S(1)}, u32[]{:S(2)}, u32[]{:S(2)}) async-start(bf16[32,24,1024]{2,1,0:T(8,128)(2,1)} %bitcast.57), calls=%async_computation | async-start | bytes 3145728 | tf_op jit(solution)/shard_map/all_to_all | solution.py:332
  57.8 50.2 %collective-permute-start.10 = (bf16[128,3712]{1,0:T(8,128)(2,1)}, bf16[128,3712]{1,0:T(8,128)(2,1)S(1)}, u32[]{:S(2)}, u32[]{:S(2)}) collective-permute-start(bf16[128,3712]{1,0:T(8,128)(2,1)} %collective-permute-done.5.refs_0_), channel_id=1, source_target_pairs={{0,1},{1,2},{2,3},{3,4},{4,5},{5,6},{6,7},{7,0},{8,9},{9,10},{10,1... | collective-permute-start | bytes 2850824 | tf_op jit(solution)/shard_map/ppermute | solution.py:300
  61.2 49.9 %collective-permute-start.11 = (bf16[128,3712]{1,0:T(8,128)(2,1)}, bf16[128,3712]{1,0:T(8,128)(2,1)}, u32[]{:S(2)}, u32[]{:S(2)}) collective-permute-start(bf16[128,3712]{1,0:T(8,128)(2,1)} %collective-permute-done.6.refs_1_), channel_id=1, source_target_pairs={{0,7},{1,0},{2,1},{3,2},{4,3},{5,4},{6,5},{7,6},{8,15},{9,8},{10,9... | collective-permute-start | bytes 2850824 | tf_op jit(solution)/shard_map/ppermute | solution.py:300
  70.9 28.4 %collective-permute-start.2 = (bf16[3,24,3584]{2,1,0:T(8,128)(2,1)S(1)}, bf16[3,24,3584]{2,1,0:T(8,128)(2,1)S(1)}, u32[]{:S(2)}, u32[]{:S(2)}) collective-permute-start(bf16[3,24,3584]{2,1,0:T(8,128)(2,1)S(1)} %get-tuple-element.30), channel_id=1, source_target_pairs={{0,8},{8,16},{16,24},{24,0},{1,9},{9,17},{17,25},{25,1},{2,10},{10... | collective-permute-start | bytes 1548296 | tf_op jit(solution)/shard_map/ppermute | solution.py:300
  72.5 43.3 %collective-permute-start.3 = (bf16[3,24,3584]{2,1,0:T(8,128)(2,1)S(1)}, bf16[3,24,3584]{2,1,0:T(8,128)(2,1)S(1)}, u32[]{:S(2)}, u32[]{:S(2)}) collective-permute-start(bf16[3,24,3584]{2,1,0:T(8,128)(2,1)S(1)} %get-tuple-element.31), channel_id=1, source_target_pairs={{0,16},{8,24},{16,0},{24,8},{1,17},{9,25},{17,1},{25,9},{2,18},{10... | collective-permute-start | bytes 1548296 | tf_op jit(solution)/shard_map/ppermute | solution.py:300
  75.4 41.4 %collective-permute-start.4 = (bf16[3,24,3584]{2,1,0:T(8,128)(2,1)S(1)}, bf16[3,24,3584]{2,1,0:T(8,128)(2,1)S(1)}, u32[]{:S(2)}, u32[]{:S(2)}) collective-permute-start(bf16[3,24,3584]{2,1,0:T(8,128)(2,1)S(1)} %get-tuple-element.32), channel_id=1, source_target_pairs={{0,24},{8,0},{16,8},{24,16},{1,25},{9,1},{17,9},{25,17},{2,26},{10... | collective-permute-start | bytes 1548296 | tf_op jit(solution)/shard_map/ppermute | solution.py:300
  99.3 22.8 %copy-start.12 = (bf16[3,24,3584]{2,1,0:T(8,128)(2,1)}, bf16[3,24,3584]{2,1,0:T(8,128)(2,1)S(1)}, u32[]{:S(2)}) copy-start(bf16[3,24,3584]{2,1,0:T(8,128)(2,1)S(1)} %collective-permute-done.2.refs_1_) | copy-start | bytes 1548292
  99.3 18.4 %collective-permute-start.7 = (bf16[2,24,3584]{2,1,0:T(8,128)(2,1)S(1)}, bf16[2,24,3584]{2,1,0:T(8,128)(2,1)S(1)}, u32[]{:S(2)}, u32[]{:S(2)}) collective-permute-start(bf16[2,24,3584]{2,1,0:T(8,128)(2,1)S(1)} %get-tuple-element.36), channel_id=1, source_target_pairs={{0,8},{8,16},{16,24},{24,0},{1,9},{9,17},{17,25},{25,1},{2,10},{10... | collective-permute-start | bytes 1032200 | tf_op jit(solution)/shard_map/ppermute | solution.py:300
  107.9 14.2 %collective-permute-start.8 = (bf16[2,24,3584]{2,1,0:T(8,128)(2,1)S(1)}, bf16[2,24,3584]{2,1,0:T(8,128)(2,1)S(1)}, u32[]{:S(2)}, u32[]{:S(2)}) collective-permute-start(bf16[2,24,3584]{2,1,0:T(8,128)(2,1)S(1)} %get-tuple-element.37), channel_id=1, source_target_pairs={{0,16},{8,24},{16,0},{24,8},{1,17},{9,25},{17,1},{25,9},{2,18},{10... | collective-permute-start | bytes 1032200 | tf_op jit(solution)/shard_map/ppermute | solution.py:300
  111.1 17.0 %collective-permute-start.9 = (bf16[2,24,3584]{2,1,0:T(8,128)(2,1)S(1)}, bf16[2,24,3584]{2,1,0:T(8,128)(2,1)S(1)}, u32[]{:S(2)}, u32[]{:S(2)}) collective-permute-start(bf16[2,24,3584]{2,1,0:T(8,128)(2,1)S(1)} %get-tuple-element.38), channel_id=1, source_target_pairs={{0,24},{8,0},{16,8},{24,16},{1,25},{9,1},{17,9},{25,17},{2,26},{10... | collective-permute-start | bytes 1032200 | tf_op jit(solution)/shard_map/ppermute | solution.py:300
  115.8 23.9 %collective-permute-start.12 = (bf16[2,24,3584]{2,1,0:T(8,128)(2,1)}, bf16[2,24,3584]{2,1,0:T(8,128)(2,1)}, u32[]{:S(2)}, u32[]{:S(2)}) collective-permute-start(bf16[2,24,3584]{2,1,0:T(8,128)(2,1)} %get-tuple-element.40), channel_id=1, source_target_pairs={{0,8},{8,16},{16,24},{24,0},{1,9},{9,17},{17,25},{25,1},{2,10},{10... | collective-permute-start | bytes 1032200 | tf_op jit(solution)/shard_map/ppermute | solution.py:300
  116.8 22.8 %collective-permute-start.13 = (bf16[2,24,3584]{2,1,0:T(8,128)(2,1)}, bf16[2,24,3584]{2,1,0:T(8,128)(2,1)}, u32[]{:S(2)}, u32[]{:S(2)}) collective-permute-start(bf16[2,24,3584]{2,1,0:T(8,128)(2,1)} %get-tuple-element.41), channel_id=1, source_target_pairs={{0,16},{8,24},{16,0},{24,8},{1,17},{9,25},{17,1},{25,9},{2,18},{10... | collective-permute-start | bytes 1032200 | tf_op jit(solution)/shard_map/ppermute | solution.py:300
  117.7 22.8 %collective-permute-start.14 = (bf16[2,24,3584]{2,1,0:T(8,128)(2,1)}, bf16[2,24,3584]{2,1,0:T(8,128)(2,1)}, u32[]{:S(2)}, u32[]{:S(2)}) collective-permute-start(bf16[2,24,3584]{2,1,0:T(8,128)(2,1)} %get-tuple-element.42), channel_id=1, source_target_pairs={{0,24},{8,0},{16,8},{24,16},{1,25},{9,1},{17,9},{25,17},{2,26},{10... | collective-permute-start | bytes 1032200 | tf_op jit(solution)/shard_map/ppermute | solution.py:300
  122.1 28.4 %collective-permute-start.15 = (bf16[64,3712]{1,0:T(8,128)(2,1)}, bf16[64,3712]{1,0:T(8,128)(2,1)S(1)}, u32[]{:S(2)}, u32[]{:S(2)}) collective-permute-start(bf16[64,3712]{1,0:T(8,128)(2,1)} %slice.44), channel_id=1, source_target_pairs={{0,1},{1,2},{2,3},{3,4},{4,5},{5,6},{6,7},{7,0},{8,9},{9,10},{10,1... | collective-permute-start | bytes 1425416 | tf_op jit(solution)/shard_map/ppermute | solution.py:300
  128.8 21.7 %collective-permute-start.16 = (bf16[64,3712]{1,0:T(8,128)(2,1)S(1)}, bf16[64,3712]{1,0:T(8,128)(2,1)S(1)}, u32[]{:S(2)}, u32[]{:S(2)}) collective-permute-start(bf16[64,3712]{1,0:T(8,128)(2,1)S(1)} %slice.45), channel_id=1, source_target_pairs={{0,7},{1,0},{2,1},{3,2},{4,3},{5,4},{6,5},{7,6},{8,15},{9,8},{10,9... | collective-permute-start | bytes 1425416 | tf_op jit(solution)/shard_map/ppermute | solution.py:300
  152.0 7.2 %collective-permute-start.17 = (bf16[1,24,3584]{2,1,0:T(8,128)(2,1)S(1)}, bf16[1,24,3584]{2,1,0:T(8,128)(2,1)S(1)}, u32[]{:S(2)}, u32[]{:S(2)}) collective-permute-start(bf16[1,24,3584]{2,1,0:T(8,128)(2,1)S(1)} %get-tuple-element.45), channel_id=1, source_target_pairs={{0,8},{8,16},{16,24},{24,0},{1,9},{9,17},{17,25},{25,1},{2,10},{10... | collective-permute-start | bytes 516104 | tf_op jit(solution)/shard_map/ppermute | solution.py:300
  153.3 10.9 %collective-permute-start.18 = (bf16[1,24,3584]{2,1,0:T(8,128)(2,1)S(1)}, bf16[1,24,3584]{2,1,0:T(8,128)(2,1)S(1)}, u32[]{:S(2)}, u32[]{:S(2)}) collective-permute-start(bf16[1,24,3584]{2,1,0:T(8,128)(2,1)S(1)} %get-tuple-element.46), channel_id=1, source_target_pairs={{0,16},{8,24},{16,0},{24,8},{1,17},{9,25},{17,1},{25,9},{2,18},{10... | collective-permute-start | bytes 516104 | tf_op jit(solution)/shard_map/ppermute | solution.py:300
  156.2 8.0 %collective-permute-start.19 = (bf16[1,24,3584]{2,1,0:T(8,128)(2,1)S(1)}, bf16[1,24,3584]{2,1,0:T(8,128)(2,1)S(1)}, u32[]{:S(2)}, u32[]{:S(2)}) collective-permute-start(bf16[1,24,3584]{2,1,0:T(8,128)(2,1)S(1)} %get-tuple-element.47), channel_id=1, source_target_pairs={{0,24},{8,0},{16,8},{24,16},{1,25},{9,1},{17,9},{25,17},{2,26},{10... | collective-permute-start | bytes 516104 | tf_op jit(solution)/shard_map/ppermute | solution.py:300
  183.9 7.6 %collective-permute-start.20 = (bf16[4,448,1024]{2,1,0:T(8,128)(2,1)}, bf16[4,448,1024]{2,1,0:T(8,128)(2,1)}, u32[]{:S(2)}, u32[]{:S(2)}) collective-permute-start(bf16[4,448,1024]{2,1,0:T(8,128)(2,1)} %dynamic-slice_bitcast_fusion), channel_id=1, source_target_pairs={{0,32},{32,0},{1,33},{33,1},{2,34},{34,2},{3,35},{35,3},{4,36},{36... | collective-permute-start | bytes 11010056 | tf_op jit(solution)/shard_map/ppermute | solution.py:300
  183.9 46.9 %all-to-all-start.1 = ((bf16[32,24,1024]{2,1,0:T(8,128)(2,1)}), bf16[32,24,1024]{2,1,0:T(8,128)(2,1)S(1)}, u32[]{:S(2)}, u32[]{:S(2)}) async-start(bf16[32,24,1024]{2,1,0:T(8,128)(2,1)} %bitcast.7), calls=%async_computation.1 | async-start | bytes 3145728 | tf_op jit(solution)/shard_map/all_to_all | solution.py:332
  200.2 13.4 %collective-permute-start.21 = (bf16[448,512]{1,0:T(8,128)(2,1)S(1)}, bf16[448,512]{1,0:T(8,128)(2,1)S(1)}, u32[]{:S(2)}, u32[]{:S(2)}) collective-permute-start(bf16[448,512]{1,0:T(8,128)(2,1)S(1)} %get-tuple-element.55), channel_id=1, source_target_pairs={{0,64},{64,128},{128,192},{192,0},{1,65},{65,129},{129,193},{193,1... | collective-permute-start | bytes 1376264 | tf_op jit(solution)/shard_map/ppermute | solution.py:300
  201.4 13.4 %collective-permute-start.25 = (bf16[448,512]{1,0:T(8,128)(2,1)S(1)}, bf16[448,512]{1,0:T(8,128)(2,1)S(1)}, u32[]{:S(2)}, u32[]{:S(2)}) collective-permute-start(bf16[448,512]{1,0:T(8,128)(2,1)S(1)} %get-tuple-element.53), channel_id=1, source_target_pairs={{0,192},{64,0},{128,64},{192,128},{1,193},{65,1},{129,65},{193,129... | collective-permute-start | bytes 1376264 | tf_op jit(solution)/shard_map/ppermute | solution.py:300
  202.2 30.8 %collective-permute-start.23 = (bf16[448,512]{1,0:T(8,128)(2,1)}, bf16[448,512]{1,0:T(8,128)(2,1)}, u32[]{:S(2)}, u32[]{:S(2)}) collective-permute-start(bf16[448,512]{1,0:T(8,128)(2,1)} %get-tuple-element.54), channel_id=1, source_target_pairs={{0,64},{64,128},{128,192},{192,0},{1,65},{65,129},{129,193},{193,1... | collective-permute-start | bytes 1376264 | tf_op jit(solution)/shard_map/ppermute | solution.py:300
  203.4 29.6 %collective-permute-start.24 = (bf16[448,512]{1,0:T(8,128)(2,1)}, bf16[448,512]{1,0:T(8,128)(2,1)}, u32[]{:S(2)}, u32[]{:S(2)}) collective-permute-start(bf16[448,512]{1,0:T(8,128)(2,1)} %get-tuple-element.52), channel_id=1, source_target_pairs={{0,192},{64,0},{128,64},{192,128},{1,193},{65,1},{129,65},{193,129... | collective-permute-start | bytes 1376264 | tf_op jit(solution)/shard_map/ppermute | solution.py:300
  217.1 15.9 %collective-permute-start.22 = (bf16[448,512]{1,0:T(8,128)(2,1)}, bf16[448,512]{1,0:T(8,128)(2,1)}, u32[]{:S(2)}, u32[]{:S(2)}) collective-permute-start(bf16[448,512]{1,0:T(8,128)(2,1)} %get-tuple-element.57), channel_id=1, source_target_pairs={{0,64},{64,128},{128,192},{192,0},{1,65},{65,129},{129,193},{193,1... | collective-permute-start | bytes 1376264 | tf_op jit(solution)/shard_map/ppermute | solution.py:300
  218.8 14.7 %collective-permute-start.26 = (bf16[448,512]{1,0:T(8,128)(2,1)}, bf16[448,512]{1,0:T(8,128)(2,1)}, u32[]{:S(2)}, u32[]{:S(2)}) collective-permute-start(bf16[448,512]{1,0:T(8,128)(2,1)} %get-tuple-element.56), channel_id=1, source_target_pairs={{0,192},{64,0},{128,64},{192,128},{1,193},{65,1},{129,65},{193,129... | collective-permute-start | bytes 1376264 | tf_op jit(solution)/shard_map/ppermute | solution.py:300
  (17 other events, 86.2 us)
